TPU v7x, 32 devices: a whole 2x2x4 slice. The times are simulated.
32 devices in a mesh: cls: 4 (over x, core), draw: 8 (over z, y).
Axes of the slice: x: 2, y: 2, z: 4, core: 2. Of those that a mesh axis runs over, the one named last changes fastest.
Arguments:
- features: bfloat16 [128, 1024], replicated, may hold values from -128 to 128
- mean_head: bfloat16 [1024, 21888], P('draw', 'cls'), may hold values from -1 to 1
- scale_head: bfloat16 [1024, 21888], P('draw', 'cls'), may hold values from -1 to 1
- factor: bfloat16 [21888, 50], P('cls'), may hold values from -0.875 to 0.875
- noise: bfloat16 [16, 128, 50], P('draw'), may hold values from -5 to 5
- labels: float32 [128, 21888], P(None, 'cls'), may hold values from 0 to 1, as said below
Outputs:
- mean_grad: float32 [1024, 21888], P('draw', 'cls')
- scale_grad: float32 [1024, 21888], P('draw', 'cls')
- feature_grad: float32 [128, 1024], P(None, 'draw')
Inputs may be any that keep to these rules, and one draw needn't show every extreme that they name: `labels`: each row is nonnegative, sums to one, and is zero on the last 45 classes.
All inputs are finite; a program needn't handle non-finite values.
Results may differ from a plain program's by a relative error of at most 0.0028.
Values may be sent and summed in bfloat16 or wider, within the bound.
A program may use at most 320 MiB of HBM per device.

v0:
```python
import jax
import jax.numpy as jnp
from jax import lax
from jax.sharding import PartitionSpec as P

CREAL = 21843


def on_device(features, mean_head, scale_head, factor, noise, labels):
    rows_here = mean_head.shape[0]
    columns = mean_head.shape[1]
    batch = features.shape[0]
    own_count = batch // lax.axis_size("draw")
    draw_pos = lax.axis_index("draw")
    image_start = draw_pos * own_count
    my_columns = lax.dynamic_slice_in_dim(features, draw_pos * rows_here, rows_here, 1)
    class_ids = lax.axis_index("cls") * columns + jnp.arange(columns, dtype=jnp.int32)
    shift = jnp.where(class_ids >= CREAL, 30000.0, 0.0).astype(jnp.float32)
    both_heads = jnp.concatenate((mean_head, scale_head), axis=1)
    chosen = my_columns
    both_logits = lax.psum_scatter(
        jnp.dot(chosen, both_heads, preferred_element_type=jnp.float32),
        "draw",
        scatter_dimension=0,
        tiled=True,
    )
    mean_logit = both_logits[:, :columns]
    scale_pre = both_logits[:, columns:]
    noise_local = lax.all_to_all(noise, "draw", split_axis=1, concat_axis=0, tiled=True)
    label_rows = lax.dynamic_slice_in_dim(labels, image_start, own_count, 0)
    spread = jax.nn.softplus(scale_pre)
    lowrank = lax.dot_general(
        noise_local, factor, (((2,), (1,)), ((), ())), preferred_element_type=jnp.float32
    )
    logits = mean_logit[None] + spread[None] * lowrank - shift[None, None, :]
    row_top = lax.pmax(jnp.max(logits, axis=2), "cls")
    row_total = lax.psum(jnp.sum(jnp.exp(logits - row_top[:, :, None]), axis=2), "cls")
    log_prob = logits - (row_top + jnp.log(row_total))[:, :, None]
    local_best = jnp.max(log_prob, axis=0)
    local_summed = jnp.sum(jnp.exp(log_prob - local_best[None]), axis=0)
    best, summed = (local_best, local_summed)
    mix = best + jnp.log(summed)
    ratio = jnp.exp(log_prob - mix[None])
    label_dot = lax.psum(jnp.sum(label_rows[None] * ratio, axis=2), "cls")
    logit_cot = (jnp.exp(log_prob) * label_dot[:, :, None] - label_rows[None] * ratio) / batch
    dmean = jnp.sum(logit_cot, axis=0)
    dspread = jnp.sum(logit_cot * lowrank, axis=0)
    mean_cot = dmean.astype(jnp.bfloat16)
    scale_cot = (dspread * jax.nn.sigmoid(scale_pre)).astype(jnp.bfloat16)
    pieces = (
        lax.all_gather(mean_cot, "draw", axis=0, tiled=True),
        lax.all_gather(scale_cot, "draw", axis=0, tiled=True),
    )
    chosen = my_columns
    contract = (((0,), (0,)), ((), ()))
    across = (((1,), (1,)), ((), ()))
    mean_part = lax.dot_general(chosen, pieces[0], contract, preferred_element_type=jnp.float32)
    scale_part = lax.dot_general(chosen, pieces[1], contract, preferred_element_type=jnp.float32)
    rows_part = lax.dot_general(
        pieces[0], mean_head, across, preferred_element_type=jnp.float32
    ) + lax.dot_general(pieces[1], scale_head, across, preferred_element_type=jnp.float32)
    feature_part = rows_part
    mean_grad, scale_grad, feature_part = (mean_part, scale_part, feature_part)
    feature_grad = lax.psum(feature_part, "cls")
    return (mean_grad, scale_grad, feature_grad)


def solution(mesh):
    return jax.shard_map(
        on_device,
        mesh=mesh,
        in_specs=(
            P(),
            P("draw", "cls"),
            P("draw", "cls"),
            P("cls", None),
            P("draw", None, None),
            P(None, "cls"),
        ),
        out_specs=(P("draw", "cls"), P("draw", "cls"), P(None, "draw")),
        check_vma=False,
    )
```

profile of v0, /device:TPU:9, one launch (start us, length us, event | category | flops | bytes accessed | tf_op | source)
XLA Modules:
  0.0 292.8 jit_solution(4773306250811411457)
XLA Ops:
  7.2 5.3 %fusion.2 = f32[128,10944]{1,0:T(8,128)} fusion(bf16[128,5472]{0,1:T(8,128)(2,1)} %param.8, bf16[128,5472]{0,1:T(8,128)(2,1)} %param.7, bf16[128,1024]{1,0:T(8,128)(2,1)} %param.6, s32[]{:T(128)S(6)} %select_n.18), kind=kOutput, calls=%fused_computation.9 | convolution fusion | flops 364216320 | bytes 8437764 | tf_op jit(solution)/shard_map/dot_general | solution.py:22
  13.5 5.7 %all-to-all-start = ((bf16[8,2,800]{2,1,0:T(2,128)(2,1)}), bf16[8,2,800]{2,1,0:T(2,128)(2,1)S(1)}, u32[]{:S(2)}, u32[]{:S(2)}) async-start(bf16[8,2,800]{2,1,0:T(2,128)(2,1)} %reshape.26), calls=%async_computation.1 | async-start | bytes 57344 | tf_op jit(solution)/shard_map/all_to_all | solution.py:29
  19.2 2.3 constant_dynamic-slice_fusion
  21.5 2.9 %copy.17 = f32[16,5472]{1,0:T(8,128)} copy(f32[16,5472]{0,1:T(8,128)} %constant_dynamic-slice_fusion) | data formatting | bytes 700416 | tf_op jit(solution)/shard_map/dynamic_slice | solution.py:30
  25.3 97.0 %reduce-scatter.2.cloned.1.call-done = f32[16,10944]{1,0:T(8,128)} async-done(((f32[128,10944]{1,0:T(8,128)}), f32[16,10944]{1,0:T(8,128)}) %reduce-scatter.2.cloned.1.call-update) | async-done | bytes 700432 | tf_op jit(solution)/shard_map/reduce_scatter | solution.py:21
  122.3 1.4 fusion.19
  123.6 4.6 %fusion.8 = (f32[16,16]{1,0:T(8,128)S(1)}, f32[16,16,5472]{2,1,0:T(8,128)}) fusion(f32[5472]{0:T(1024)S(1)} %fusion.9, f32[16,5472]{1,0:T(8,128)S(1)} %get-tuple-element.6, f32[16,5472]{1,0:T(8,128)S(1)} %get-tuple-element.5, bf16[16,16,50]{2,1,0:T(8,128)(2,1)} %bitcast.18, bf16[5472,50]{0,1:T(8,128)(2,1)} %param.9), kind=kOutput, calls=%fused_computation.19 | convolution fusion | flops 145686272 | bytes 6899456 | tf_op jit(solution)/shard_map/dot_general | solution.py:32
  128.2 5.9 %pmax.7 = f32[16,16]{1,0:T(8,128)S(1)} all-reduce(f32[16,16]{1,0:T(8,128)S(1)} %get-tuple-element.7), channel_id=1, replica_groups=mesh['cls'=4,'draw'=8] {'cls'}, use_global_device_ids=true, to_apply=%region_2.3 | all-reduce | flops 256 | bytes 2048 | tf_op jit(solution)/shard_map/pmax | solution.py:36
  134.2 4.2 %exponential_reduce_fusion.1 = f32[16,16]{1,0:T(8,128)S(1)} fusion(f32[16,16]{1,0:T(8,128)S(1)} %pmax.7, f32[5472]{0:T(1024)S(1)} %fusion.9, f32[16,16,5472]{2,1,0:T(8,128)} %get-tuple-element.8, f32[16,5472]{1,0:T(8,128)S(1)} %get-tuple-element.6, f32[16,5472]{1,0:T(8,128)S(1)} %get-tuple-element.5), kind=kLoop, calls=%fused_computation.4 | loop fusion | flops 7003904 | bytes 6327680 | tf_op jit(solution)/shard_map/reduce_sum | solution.py:37
  138.4 6.5 %psum.21 = f32[16,16]{1,0:T(8,128)S(1)} all-reduce(f32[16,16]{1,0:T(8,128)S(1)} %exponential_reduce_fusion.1), channel_id=1, replica_groups=mesh['cls'=4,'draw'=8] {'cls'}, use_global_device_ids=true, to_apply=%region_4.5 | all-reduce | flops 256 | bytes 2048 | tf_op jit(solution)/shard_map/psum | solution.py:37
  144.9 3.8 %subtract_reduce_fusion = f32[16,5472]{1,0:T(8,128)S(1)} fusion(f32[16,16]{1,0:T(8,128)S(1)} %log_add_fusion.1, f32[5472]{0:T(1024)S(1)} %fusion.9, f32[16,16,5472]{2,1,0:T(8,128)} %get-tuple-element.8, f32[16,5472]{1,0:T(8,128)S(1)} %get-tuple-element.6, f32[16,5472]{1,0:T(8,128)S(1)} %get-tuple-element.5), kind=kLoop, calls=%fused_computation.7 | loop fusion | flops 6916608 | bytes 6676864 | tf_op jit(solution)/shard_map/reduce_max | solution.py:39
  149.1 1.5 exponential_reduce_fusion
  151.5 2.5 fusion
  154.0 5.9 %psum.22 = f32[16,16]{1,0:T(8,128)S(1)} all-reduce(f32[16,16]{1,0:T(8,128)S(1)} %fusion), channel_id=1, replica_groups=mesh['cls'=4,'draw'=8] {'cls'}, use_global_device_ids=true, to_apply=%region_8.9 | all-reduce | flops 256 | bytes 2048 | tf_op jit(solution)/shard_map/psum | solution.py:44
  159.9 5.9 %multiply_reduce_fusion = (f32[16,5472]{1,0:T(8,128)}, bf16[16,5472]{1,0:T(8,128)(2,1)}) fusion(f32[16,16,5472]{2,1,0:T(8,128)} %get-tuple-element.8, f32[16,16]{1,0:T(8,128)S(1)} %psum.22, f32[16,5472]{1,0:T(8,128)} %copy-done.3, f32[16,5472]{1,0:T(8,128)} %copy.17, f32[16,16]{1,0:T(8,128)S(1)} %log_add_fusion.1, f32[5472]{0:T(1024)S(1)} %fusion.9, ...), kind=kLoop, calls=%fused_computation | loop fusion | flops 16634880 | bytes 7553408 | tf_op jit(solution)/shard_map/reduce_sum | solution.py:47
  166.0 1.9 multiply_convert_fusion
  168.0 40.2 %all-gather.3.cloned.1.call-done = bf16[128,5472]{1,0:T(8,128)(2,1)} async-done(((bf16[16,5472]{1,0:T(8,128)(2,1)}), bf16[128,5472]{1,0:T(8,128)(2,1)}) %all-gather.3.cloned.1.call-update) | async-done | bytes 1400848 | tf_op jit(solution)/shard_map/all_gather | solution.py:51
  208.3 2.3 fusion.20
  210.6 41.9 %all-gather.5.cloned.1.call-done = bf16[128,5472]{1,0:T(8,128)(2,1)} async-done(((bf16[16,5472]{1,0:T(8,128)(2,1)}), bf16[128,5472]{1,0:T(8,128)(2,1)}) %all-gather.5.cloned.1.call-update) | async-done | bytes 1400848 | tf_op jit(solution)/shard_map/all_gather | solution.py:52
  252.5 2.9 %convolution_add_fusion = f32[128,128]{1,0:T(8,128)} fusion(f32[128,128]{1,0:T(8,128)S(1)} %fusion.20, bf16[128,5472]{1,0:T(8,128)(2,1)} %all-gather.5.cloned.1.call-done, bf16[128,5472]{0,1:T(8,128)(2,1)} %param.8), kind=kOutput, calls=%fused_computation.13 | convolution fusion | flops 179322880 | bytes 2932736 | tf_op jit(solution)/shard_map/dot_general | solution.py:61
  255.4 3.6 %fusion.10 = f32[128,5472]{0,1:T(8,128)} fusion(bf16[128,5472]{1,0:T(8,128)(2,1)} %all-gather.5.cloned.1.call-done, bf16[128,1024]{1,0:T(8,128)(2,1)} %param.6, s32[]{:T(128)S(6)} %select_n.18), kind=kOutput, calls=%fused_computation.22 | convolution fusion | flops 179306496 | bytes 4243460 | tf_op jit(solution)/shard_map/dot_general | solution.py:58
  259.0 3.6 %fusion.12 = f32[128,5472]{0,1:T(8,128)} fusion(bf16[128,5472]{1,0:T(8,128)(2,1)} %all-gather.3.cloned.1.call-done, bf16[128,1024]{1,0:T(8,128)(2,1)} %param.6, s32[]{:T(128)S(6)} %select_n.18), kind=kOutput, calls=%fused_computation.24 | convolution fusion | flops 179306496 | bytes 4243460 | tf_op jit(solution)/shard_map/dot_general | solution.py:57
  262.6 22.2 %all-reduce.2.cloned.1.call-done = f32[128,128]{1,0:T(8,128)} async-done(((f32[128,128]{1,0:T(8,128)}), f32[128,128]{1,0:T(8,128)}) %all-reduce.2.cloned.1.call-update) | async-done | bytes 65552 | tf_op jit(solution)/shard_map/psum | solution.py:64
  284.8 1.5 copy.19
  (27 shorter events, 3.3 us)
Async XLA Ops:
  7.2 12.0 %copy-start = (f32[128,5472]{0,1:T(8,128)S(1)}, f32[128,5472]{0,1:T(8,128)}, u32[]{:S(2)}) copy-start(f32[128,5472]{0,1:T(8,128)} %param.11) | copy-start | bytes 8404996
  7.2 115.1 %reduce-scatter.2.cloned.1.call-start = ((), (), s32[]{:S(2)}) async-start(), calls=%async_computation.2 | async-start | bytes 6340608 | tf_op jit(solution)/shard_map/reduce_scatter | solution.py:21
  7.2 5.3 %copy-start.4 = (bf16[2,128,50]{1,0,2:T(2,128)(2,1)S(1)}, bf16[2,128,50]{1,0,2:T(2,128)(2,1)}, u32[]{:S(2)}) copy-start(bf16[2,128,50]{1,0,2:T(2,128)(2,1)} %param.10) | copy-start | bytes 76804
  13.5 11.0 %all-to-all-start = ((bf16[8,2,800]{2,1,0:T(2,128)(2,1)}), bf16[8,2,800]{2,1,0:T(2,128)(2,1)S(1)}, u32[]{:S(2)}, u32[]{:S(2)}) async-start(bf16[8,2,800]{2,1,0:T(2,128)(2,1)} %reshape.26), calls=%async_computation.1 | async-start | bytes 57344 | tf_op jit(solution)/shard_map/all_to_all | solution.py:29
  19.2 189.1 %all-gather.3.cloned.1.call-start = ((), (), s32[]{:S(2)}) async-start(), calls=%async_computation.3 | async-start | bytes 1585152 | tf_op jit(solution)/shard_map/all_gather | solution.py:51
  144.9 4.3 %copy-start.1 = (f32[16,16,5472]{2,1,0:T(8,128)S(1)}, f32[16,16,5472]{2,1,0:T(8,128)}, u32[]{:S(2)}) copy-start(f32[16,16,5472]{2,1,0:T(8,128)} %get-tuple-element.8) | copy-start | bytes 16809988
  149.1 2.3 copy-start.2
  150.7 0.7 copy-start.3
  165.8 86.7 %all-gather.5.cloned.1.call-start = ((), (), s32[]{:S(2)}) async-start(), calls=%async_computation.4 | async-start | bytes 1585152 | tf_op jit(solution)/shard_map/all_gather | solution.py:52
  168.0 116.8 %all-reduce.2.cloned.1.call-start = ((), (), s32[]{:S(2)}) async-start(), calls=%async_computation.5 | async-start | bytes 131072 | tf_op jit(solution)/shard_map/psum | solution.py:64
Sparse Core Ops, SparseCore 0:
  12.7 109.5 reduce-scatter.1
  165.9 42.3 all-gather.2
  211.0 41.4 all-gather.4
  255.5 29.2 all-reduce.1
where the time goes:
time: 296 us; the launch traced here: 293 us
  waiting for transfers between devices  201 us (68%)
  matrix products  22.3 us (8%)
  other arithmetic  21.3 us (7%)
  blocking collectives  18.3 us (6%)
  between operations  13.9 us (5%)
  local copies, waits for them, and re-layouts  9.63 us (3%)
  starting transfers between devices  6.02 us (2%)
    reduce_scatter x1, waiting for transfers between devices, on_device(): lax.psum_scatter(jnp.dot(chosen, both_heads, preferred_element_type=jnp.f...  97 us
    all_gather x1, waiting for transfers between devices, on_device(): lax.all_gather(scale_cot, 'draw', axis=0, tiled=True)  41.9 us
    all_gather x1, waiting for transfers between devices, on_device(): lax.all_gather(mean_cot, 'draw', axis=0, tiled=True)  40.2 us
    psum x1, waiting for transfers between devices, on_device(): feature_grad = lax.psum(feature_part, 'cls')  22.2 us
    psum x1, blocking collectives, on_device(): lax.psum(jnp.sum(jnp.exp(logits - row_top[:, :, None]), axis=2), 'cls')  6.45 us
    pmax x1, blocking collectives, on_device(): row_top = lax.pmax(jnp.max(logits, axis=2), 'cls')  5.93 us
  transfers between devices with their start and end apart: 5, of which 4 were waited for; matrix products, arithmetic and copies ran while one was open for 6% of the time, Pallas kernels for 0%

commit v1 on v0

v1 whole, which is shorter than its diff:
```python
import functools
import jax
import jax.numpy as jnp
from jax import lax
from jax.experimental import pallas as pl
from jax.experimental.pallas import tpu as pltpu
from jax.sharding import PartitionSpec as P

CREAL = 21843
MESH = pl.DeviceIdType.MESH
ANY = pl.BlockSpec(memory_space=pl.ANY)
VMEM = pl.BlockSpec(memory_space=pltpu.VMEM)


def at_width(owner, full, part, tile, run):
    @pl.when(owner < full)
    def _():
        run(tile)

    if part:

        @pl.when(owner == full)
        def _():
            run(part)


def exchange_kernel(n, tile, full, part, mean, scale, noise, out, noise_out, send, recv, nsend, nrecv, local):
    me, cls = lax.axis_index("draw"), lax.axis_index("cls")
    rows = mean.shape[0]
    barrier = pltpu.get_barrier_semaphore()
    for k in range(1, n):
        pl.semaphore_signal(barrier, inc=1, device_id=(cls, lax.rem(me + k, n)), device_id_type=MESH)
    pl.semaphore_wait(barrier, n - 1)

    def noise_copy(slot, k, device):
        return pltpu.make_async_remote_copy(
            noise, noise_out.at[slot], nsend.at[k], nrecv.at[slot], device_id=(cls, device), device_id_type=MESH
        )

    def block_copy(head, owner, k, width, source, device):
        ref = (mean, scale)[head]
        start = pl.multiple_of(owner * tile, 128)
        return pltpu.make_async_remote_copy(
            ref.at[:, pl.ds(start, width)],
            out.at[head, pl.ds(pl.multiple_of(source * rows, rows), rows), pl.ds(0, width)],
            send.at[head, k],
            recv.at[head, source],
            device_id=(cls, device),
            device_id_type=MESH,
        )

    def own_copy(head, width):
        ref = (mean, scale)[head]
        return pltpu.make_async_copy(
            ref.at[:, pl.ds(pl.multiple_of(me * tile, 128), width)],
            out.at[head, pl.ds(pl.multiple_of(me * rows, rows), rows), pl.ds(0, width)],
            local.at[head],
        )

    own_noise = pltpu.make_async_copy(noise, noise_out.at[me], local.at[2])
    for k in range(1, n):
        to = lax.rem(me + k, n)
        for head in range(2):
            at_width(to, full, part, tile, lambda w: block_copy(head, to, k, w, me, to).start())
    for k in range(1, n):
        to = lax.rem(me + k, n)
        noise_copy(me, k, to).start()
    own_noise.start()
    for head in range(2):
        at_width(me, full, part, tile, lambda w: own_copy(head, w).start())
    for k in range(1, n):
        source = lax.rem(me + n - k, n)
        for head in range(2):
            at_width(me, full, part, tile, lambda w: block_copy(head, me, k, w, source, source).wait_recv())
        noise_copy(source, k, source).wait_recv()
    for k in range(1, n):
        to = lax.rem(me + k, n)
        for head in range(2):
            at_width(to, full, part, tile, lambda w: block_copy(head, to, k, w, me, to).wait_send())
        noise_copy(me, k, to).wait_send()
    own_noise.wait()
    for head in range(2):
        at_width(me, full, part, tile, lambda w: own_copy(head, w).wait())


def gather_kernel(n, tile, full, part, cot, out, send, recv, local):
    me, cls = lax.axis_index("draw"), lax.axis_index("cls")
    half = n // 2
    group, side = lax.div(me, 2), lax.rem(me, 2)
    partner = group * 2 + 1 - side
    barrier = pltpu.get_barrier_semaphore()
    peers = [partner] + [lax.rem(group + k, half) * 2 + side for k in range(1, half)]
    for peer in peers:
        pl.semaphore_signal(barrier, inc=1, device_id=(cls, peer), device_id_type=MESH)
    pl.semaphore_wait(barrier, half)

    def place(owner, width):
        return out.at[:, :, pl.ds(pl.multiple_of(owner * tile, 128), width)]

    def from_cot(owner, slot, width, device):
        return pltpu.make_async_remote_copy(
            cot.at[:, :, pl.ds(0, width)], place(owner, width), send.at[slot], recv.at[owner],
            device_id=(cls, device), device_id_type=MESH,
        )

    def forward(owner, slot, width, device):
        return pltpu.make_async_remote_copy(
            place(owner, width), place(owner, width), send.at[slot], recv.at[owner],
            device_id=(cls, device), device_id_type=MESH,
        )

    def own_copy(width):
        return pltpu.make_async_copy(cot.at[:, :, pl.ds(0, width)], place(me, width), local)

    for k in range(1, half):
        at_width(me, full, part, tile, lambda w: from_cot(me, k, w, peers[k]).start())
    at_width(me, full, part, tile, lambda w: from_cot(me, 0, w, partner).start())
    at_width(me, full, part, tile, lambda w: own_copy(w).start())
    order = sorted(range(1, half), key=lambda k: min(k, half - k))
    for k in order:
        owner = peers[k]
        at_width(owner, full, part, tile, lambda w: from_cot(owner, k, w, owner).wait_recv())
        at_width(owner, full, part, tile, lambda w: forward(owner, half + k, w, partner).start())
    at_width(partner, full, part, tile, lambda w: from_cot(partner, 0, w, partner).wait_recv())
    for k in range(1, half):
        owner = lax.rem(group + k, half) * 2 + 1 - side
        at_width(owner, full, part, tile, lambda w: forward(owner, half + k, w, partner).wait_recv())
    for k in range(half):
        at_width(me, full, part, tile, lambda w: from_cot(me, k, w, partner).wait_send())
    for k in range(1, half):
        owner = peers[k]
        at_width(owner, full, part, tile, lambda w: forward(owner, half + k, w, partner).wait_send())
    at_width(me, full, part, tile, lambda w: own_copy(w).wait())


def merge(slots, count, softmax):
    if not softmax:
        total = slots[0]
        for i in range(1, count):
            total = total + slots[i]
        return total
    top = slots[0, 0]
    for i in range(1, count):
        top = jnp.maximum(top, slots[i, 0])
    total = jnp.zeros_like(top)
    for i in range(count):
        total = total + slots[i, 1] * jnp.exp(slots[i, 0] - top)
    return jnp.stack((top, total))


def reduce_kernel(counts, softmax, x, out, *scratch):
    levels = len(counts)
    slots, sends, recvs = scratch[:levels], scratch[levels : 2 * levels], scratch[2 * levels :]
    cls, draw = lax.axis_index("cls"), lax.axis_index("draw")

    def device(level, index):
        return (index, draw) if level == 0 else (cls, index)

    barrier = pltpu.get_barrier_semaphore()
    for level, n in enumerate(counts):
        me = (cls, draw)[level]
        for k in range(1, n):
            pl.semaphore_signal(
                barrier, inc=1, device_id=device(level, lax.rem(me + k, n)), device_id_type=MESH
            )
    pl.semaphore_wait(barrier, sum(counts) - levels)
    value = x[...]
    for level, n in enumerate(counts):
        me = (cls, draw)[level]
        held = slots[level]
        held[me] = value

        def copy(slot, k, target):
            return pltpu.make_async_remote_copy(
                held.at[slot], held.at[slot], sends[level].at[k], recvs[level].at[slot],
                device_id=device(level, target), device_id_type=MESH,
            )

        for k in range(1, n):
            copy(me, k, lax.rem(me + k, n)).start()
        for k in range(1, n):
            source = lax.rem(me + n - k, n)
            copy(source, k, source).wait_recv()
        for k in range(1, n):
            copy(me, k, lax.rem(me + k, n)).wait_send()
        value = merge(held, n, softmax)
    if softmax:
        out[...] = value[0] + jnp.log(value[1])
    else:
        out[...] = value


def params(collective_id):
    return pltpu.CompilerParams(
        collective_id=collective_id, has_side_effects=True, vmem_limit_bytes=32 * 2**20
    )


def reduce_over(x, counts, softmax, collective_id):
    shape = x.shape[1:] if softmax else x.shape
    return pl.pallas_call(
        functools.partial(reduce_kernel, counts, softmax),
        out_shape=jax.ShapeDtypeStruct(shape, jnp.float32),
        in_specs=[VMEM],
        out_specs=VMEM,
        scratch_shapes=[pltpu.VMEM((n,) + x.shape, jnp.float32) for n in counts]
        + [pltpu.SemaphoreType.DMA((n,)) for n in counts]
        + [pltpu.SemaphoreType.DMA((n,)) for n in counts],
        compiler_params=params(collective_id),
    )(x)


def on_device(features, mean_head, scale_head, factor, noise, labels):
    rows, columns = mean_head.shape
    batch = features.shape[0]
    n, ncls = lax.axis_size("draw"), lax.axis_size("cls")
    me = lax.axis_index("draw")
    tiles = -(-columns // 128)
    tile = -(-tiles // n) * 128
    full, part = (tiles * 128) // tile, (tiles * 128) % tile
    padded = n * tile
    own, rank = noise.shape[0], noise.shape[2]
    draws = own * n
    widen = lambda a: jnp.pad(a, ((0, 0), (0, padded - columns)))

    heads, noise_t = pl.pallas_call(
        functools.partial(exchange_kernel, n, tile, full, part),
        out_shape=(
            jax.ShapeDtypeStruct((2, n * rows, tile), jnp.bfloat16),
            jax.ShapeDtypeStruct((n, own, rank, batch), jnp.bfloat16),
        ),
        in_specs=[ANY, ANY, ANY],
        out_specs=(ANY, ANY),
        scratch_shapes=[
            pltpu.SemaphoreType.DMA((2, n)),
            pltpu.SemaphoreType.DMA((2, n)),
            pltpu.SemaphoreType.DMA((n,)),
            pltpu.SemaphoreType.DMA((n,)),
            pltpu.SemaphoreType.DMA((3,)),
        ],
        compiler_params=params(0),
    )(widen(mean_head), widen(scale_head), noise.transpose(0, 2, 1))

    first = me * tile
    local_ids = first + jnp.arange(tile, dtype=jnp.int32)
    valid = local_ids < columns
    class_ids = lax.axis_index("cls") * columns + local_ids
    shift = jnp.where(class_ids >= CREAL, 30000.0, 0.0).astype(jnp.float32)
    my_factor = lax.dynamic_slice_in_dim(jnp.pad(factor, ((0, padded - columns), (0, 0))), first, tile, 0)
    my_labels = lax.dynamic_slice_in_dim(widen(labels), first, tile, 1)

    mean_logit = jnp.dot(features, heads[0], preferred_element_type=jnp.float32)
    scale_pre = jnp.dot(features, heads[1], preferred_element_type=jnp.float32)
    scale_pre = jnp.where(valid[None], scale_pre, 0.0)
    spread = jax.nn.softplus(scale_pre)
    lowrank = lax.dot_general(
        noise_t.reshape(draws, rank, batch), my_factor, (((1,), (1,)), ((), ())), preferred_element_type=jnp.float32
    )
    logits = mean_logit[None] + spread[None] * lowrank - shift[None, None, :]
    logits = jnp.where(valid[None, None, :], logits, -1e30)
    local_top = jnp.max(logits, axis=2)
    local_total = jnp.sum(jnp.exp(logits - local_top[:, :, None]), axis=2)
    lse = reduce_over(jnp.stack((local_top, local_total)), (ncls, n), True, 1)
    log_prob = logits - lse[:, :, None]
    best = jnp.max(log_prob, axis=0)
    mix = best + jnp.log(jnp.sum(jnp.exp(log_prob - best[None]), axis=0))
    ratio = jnp.exp(log_prob - mix[None])
    label_dot = reduce_over(jnp.sum(my_labels[None] * ratio, axis=2), (ncls, n), False, 2)
    logit_cot = (jnp.exp(log_prob) * label_dot[:, :, None] - my_labels[None] * ratio) / batch
    dmean = jnp.sum(logit_cot, axis=0)
    dspread = jnp.sum(logit_cot * lowrank, axis=0)
    cots = jnp.stack((dmean, dspread * jax.nn.sigmoid(scale_pre))).astype(jnp.bfloat16)

    gathered = pl.pallas_call(
        functools.partial(gather_kernel, n, tile, full, part),
        out_shape=jax.ShapeDtypeStruct((2, batch, padded), jnp.bfloat16),
        in_specs=[ANY],
        out_specs=ANY,
        scratch_shapes=[
            pltpu.SemaphoreType.DMA((n,)),
            pltpu.SemaphoreType.DMA((n,)),
            pltpu.SemaphoreType.DMA,
        ],
        compiler_params=params(3),
    )(cots)
    mean_cot, scale_cot = gathered[0, :, :columns], gathered[1, :, :columns]
    my_columns = lax.dynamic_slice_in_dim(features, me * rows, rows, 1)
    contract = (((0,), (0,)), ((), ()))
    across = (((1,), (1,)), ((), ()))
    feature_part = lax.dot_general(
        mean_cot, mean_head, across, preferred_element_type=jnp.float32
    ) + lax.dot_general(scale_cot, scale_head, across, preferred_element_type=jnp.float32)
    mean_grad = lax.dot_general(my_columns, mean_cot, contract, preferred_element_type=jnp.float32)
    scale_grad = lax.dot_general(my_columns, scale_cot, contract, preferred_element_type=jnp.float32)
    feature_grad = reduce_over(feature_part, (ncls,), False, 4)
    return (mean_grad, scale_grad, feature_grad)


def solution(mesh):
    return jax.shard_map(
        on_device,
        mesh=mesh,
        in_specs=(
            P(),
            P("draw", "cls"),
            P("draw", "cls"),
            P("cls", None),
            P("draw", None, None),
            P(None, "cls"),
        ),
        out_specs=(P("draw", "cls"), P("draw", "cls"), P(None, "draw")),
        check_vma=False,
    )
```

time: 296 us -> 196 us (0.66)
  waiting for transfers between devices: 201 us -> 0 us
  Pallas kernels: 0 us -> 164 us
  blocking collectives: 18.3 us -> 0 us
  matrix products: 22.3 us -> 8.42 us
  between operations: 13.9 us -> 0.9 us
  other arithmetic: 21.3 us -> 13 us
  starting transfers between devices: 6.02 us -> 0 us
    pallas_call x0 -> x5, Pallas kernels: none -> 164 us  [the longest x1 77 us: on_device(): pl.pallas_call(functools.partial(exchange_kernel, n, tile, full, part), o...]
    reduce_scatter x1 -> x0, waiting for transfers between devices: 97 us -> none  [on_device(): lax.psum_scatter(jnp.dot(chosen, both_heads, preferred_element_type=jnp.f...]
    all_gather x2 -> x0, waiting for transfers between devices: 82.1 us -> none  [the longest x1 41.9 us: on_device(): lax.all_gather(scale_cot, 'draw', axis=0, tiled=True)]
    psum x1 -> x0, waiting for transfers between devices: 22.2 us -> none  [on_device(): feature_grad = lax.psum(feature_part, 'cls')]
    dot_general x6 -> x7, matrix products: 22.3 us -> 8.42 us  [the longest x1 2.23 us: on_device(): lax.dot_general(my_columns, scale_cot, contract, preferred_element_type=j...]
    psum x2 -> x0, blocking collectives: 12.4 us -> none  [the longest x1 6.45 us: on_device(): lax.psum(jnp.sum(jnp.exp(logits - row_top[:, :, None]), axis=2), 'cls')]
    pmax x1 -> x0, blocking collectives: 5.93 us -> none  [on_device(): row_top = lax.pmax(jnp.max(logits, axis=2), 'cls')]
    all_to_all x1 -> x0, starting transfers between devices: 5.72 us -> none  [on_device(): lax.all_to_all(noise, 'draw', split_axis=1, concat_axis=0, tiled=True)]
  transfers between devices with their start and end apart: 5 -> 0, of which waited for: 4 -> 0; matrix products, arithmetic and copies ran while one was open for 6% -> 0% of each run, Pallas kernels for 0% -> 0%
where the time goes in v1:
time: 196 us; the launch traced here: 194 us
  Pallas kernels  164 us (84%)
  other arithmetic  13 us (7%)
  matrix products  8.42 us (4%)
  local copies, waits for them, and re-layouts  7.59 us (4%)
    pallas_call x1, Pallas kernels, on_device(): pl.pallas_call(functools.partial(exchange_kernel, n, tile, full, part), o...  77 us
    pallas_call x1, Pallas kernels, on_device(): pl.pallas_call(functools.partial(gather_kernel, n, tile, full, part), out...  61.6 us
    pallas_call x3, Pallas kernels, reduce_over(): pl.pallas_call(functools.partial(reduce_kernel, counts, softmax), out_sha...  25.9 us
    unnamed x14, local copies, waits for them, and re-layouts  5.11 us
    reduce_sum x1, other arithmetic, on_device(): dmean = jnp.sum(logit_cot, axis=0)  4.77 us

profile of v1, /device:TPU:9, one launch (start us, length us, event | category | flops | bytes accessed | tf_op | source)
XLA Modules:
  0.0 194.4 jit_solution(18161446539828871805)
XLA Ops:
  0.7 0.8 copy.17
  1.5 1.1 pad_dynamic-slice_fusion
  2.6 0.9 copy.14
  3.5 1.8 copy.9
  5.5 1.8 copy.10
  7.5 77.0 %shard_map.85 = (bf16[2,1024,768]{2,1,0:T(8,128)(2,1)S(1)}, bf16[8,2,50,128]{3,2,1,0:T(8,128)(2,1)S(1)}) custom-call(bf16[128,6144]{1,0:T(8,128)(2,1)S(1)} %pad.15.mean, bf16[128,6144]{1,0:T(8,128)(2,1)S(1)} %pad.16.scale, bf16[2,50,128]{2,1,0:T(8,128)(2,1)S(1)} %bitcast.52), custom_call_target="tpu_custom_call" | custom-call | tf_op jit(solution)/shard_map/pallas_call | solution.py:226
  84.5 0.6 fusion.20
  85.1 0.5 compare_select_fusion
  85.7 0.2 copy.12
  85.9 1.7 fusion.43
  87.6 2.0 %exponential_reduce_fusion.1 = f32[16,128]{1,0:T(8,128)S(1)} fusion(f32[16,128]{1,0:T(8,128)S(1)} %get-tuple-element.11, f32[768]{0:T(1024)S(1)} %fusion.38, f32[16,128,768]{2,1,0:T(8,128)S(1)} %get-tuple-element.12, f32[128,768]{1,0:T(8,128)S(1)} %get-tuple-element.9, f32[128,768]{1,0:T(8,128)S(1)} %copy.12, pred[768]{0:T(1024)(128)(4,1)S(1)} %fusion.37), kind=kLoop, calls=%fused_computation.4 | loop fusion | flops 9435136 | bytes 7098112 | tf_op jit(solution)/shard_map/reduce_sum | solution.py:262
  89.6 9.3 %shard_map.86 = f32[16,128]{1,0:T(8,128)S(1)} custom-call(f32[2,16,128]{2,1,0:T(8,128)S(1)} %pad_maximum_fusion.1.x), custom_call_target="tpu_custom_call" | custom-call | tf_op jit(solution)/shard_map/pallas_call | solution.py:201
  98.9 1.4 subtract_reduce_fusion
  100.4 2.2 %exponential_reduce_fusion = f32[128,768]{1,0:T(8,128)S(1)} fusion(f32[128,768]{1,0:T(8,128)S(1)} %subtract_reduce_fusion, f32[16,128]{1,0:T(8,128)S(1)} %shard_map.86, f32[768]{0:T(1024)S(1)} %fusion.38, f32[16,128,768]{2,1,0:T(8,128)S(1)} %get-tuple-element.12, f32[128,768]{1,0:T(8,128)S(1)} %get-tuple-element.9, f32[128,768]{1,0:T(8,128)S(1)} %copy.12, ...), kind=kLoop, calls=%fused_computation.3 | loop fusion | flops 10911744 | bytes 7876352 | tf_op jit(solution)/shard_map/reduce_sum | solution.py:266
  102.6 2.5 %fusion.x = f32[16,128]{1,0:T(8,128)S(1)} fusion(f32[128,768]{1,0:T(8,128)S(1)} %log_add_fusion, f32[128,768]{1,0:T(8,128)S(1)} %copy-done.1, f32[16,128]{1,0:T(8,128)S(1)} %shard_map.86, f32[768]{0:T(1024)S(1)} %fusion.38, f32[16,128,768]{2,1,0:T(8,128)S(1)} %get-tuple-element.12, f32[128,768]{1,0:T(8,128)S(1)} %get-tuple-element.9, ...), kind=kLoop, calls=%fused_computation.6 | loop fusion | flops 12580864 | bytes 7884544 | tf_op jit(solution)/shard_map/reduce_sum | solution.py:268
  105.1 9.7 %shard_map.87 = f32[16,128]{1,0:T(8,128)S(1)} custom-call(f32[16,128]{1,0:T(8,128)S(1)} %fusion.x), custom_call_target="tpu_custom_call" | custom-call | tf_op jit(solution)/shard_map/pallas_call | solution.py:201
  114.8 4.8 %fusion.1 = (bf16[128,768]{1,0:T(8,128)(2,1)S(1)}, f32[128,768]{1,0:T(8,128)S(1)}) fusion(f32[16,128]{1,0:T(8,128)S(1)} %shard_map.87, f32[128,768]{1,0:T(8,128)S(1)} %log_add_fusion, f32[128,768]{1,0:T(8,128)S(1)} %copy-done.1, f32[16,128]{1,0:T(8,128)S(1)} %shard_map.86, f32[768]{0:T(1024)S(1)} %fusion.38, f32[16,128,768]{2,1,0:T(8,128)S(1)} %get-tuple-element.12, ...), kind=kLoop, calls=%fused_computation.8 | loop fusion | flops 20250624 | bytes 8474368 | tf_op jit(solution)/shard_map/reduce_sum | solution.py:270
  119.8 61.6 %shard_map.88 = bf16[2,128,6144]{2,1,0:T(8,128)(2,1)S(1)} custom-call(bf16[2,128,768]{2,1,0:T(8,128)(2,1)S(1)} %pad_maximum_fusion.cot), custom_call_target="tpu_custom_call" | custom-call | tf_op jit(solution)/shard_map/pallas_call | solution.py:274
  181.4 0.6 fusion.8
  181.9 0.5 fusion.29.x
  182.5 6.9 %shard_map.89 = f32[128,128]{1,0:T(8,128)S(1)} custom-call(f32[128,128]{1,0:T(8,128)S(1)} %fusion.29.x), custom_call_target="tpu_custom_call" | custom-call | tf_op jit(solution)/shard_map/pallas_call | solution.py:201
  189.4 2.2 %fusion.10 = f32[128,5472]{0,1:T(8,128)} fusion(bf16[2,128,6144]{2,1,0:T(8,128)(2,1)S(1)} %shard_map.88, bf16[128,1024]{1,0:T(8,128)(2,1)S(1)} %copy-done, s32[]{:T(128)S(6)} %select_n.30), kind=kOutput, calls=%fused_computation.18 | convolution fusion | flops 179306496 | bytes 4243460 | tf_op jit(solution)/shard_map/dot_general | solution.py:294
  191.6 2.2 %fusion.14 = f32[128,5472]{0,1:T(8,128)} fusion(bf16[2,128,6144]{2,1,0:T(8,128)(2,1)S(1)} %shard_map.88, bf16[128,1024]{1,0:T(8,128)(2,1)S(1)} %copy-done, s32[]{:T(128)S(6)} %select_n.30), kind=kOutput, calls=%fused_computation.22 | convolution fusion | flops 179306496 | bytes 4243460 | tf_op jit(solution)/shard_map/dot_general | solution.py:293
  193.8 0.6 copy.19
  (18 shorter events, 0.6 us)
Async XLA Ops:
  0.6 83.9 %copy-start = (bf16[128,1024]{1,0:T(8,128)(2,1)S(1)}, bf16[128,1024]{1,0:T(8,128)(2,1)}, u32[]{:S(2)}) copy-start(bf16[128,1024]{1,0:T(8,128)(2,1)} %param.6) | copy-start | bytes 786436
  7.5 78.4 %copy-start.4 = (bf16[5472,50]{0,1:T(8,128)(2,1)S(1)}, bf16[5472,50]{0,1:T(8,128)(2,1)}, u32[]{:S(2)}) copy-start(bf16[5472,50]{0,1:T(8,128)(2,1)} %param.9) | copy-start | bytes 1641604
  100.4 2.2 %copy-start.1 = (f32[128,768]{1,0:T(8,128)S(1)}, f32[128,768]{1,0:T(8,128)}, u32[]{:S(2)}) copy-start(f32[128,768]{1,0:T(8,128)} %copy.14) | copy-start | bytes 1179652
  114.8 66.6 %copy-start.2 = (bf16[128,5472]{0,1:T(8,128)(2,1)S(1)}, bf16[128,5472]{0,1:T(8,128)(2,1)}, u32[]{:S(2)}) copy-start(bf16[128,5472]{0,1:T(8,128)(2,1)} %param.8) | copy-start | bytes 4202500
  114.8 67.1 %copy-start.3 = (bf16[128,5472]{0,1:T(8,128)(2,1)S(1)}, bf16[128,5472]{0,1:T(8,128)(2,1)}, u32[]{:S(2)}) copy-start(bf16[128,5472]{0,1:T(8,128)(2,1)} %param.7) | copy-start | bytes 4202500

commit v2 on v1

v2 whole, which is shorter than its diff:
```python
import functools
import jax
import jax.numpy as jnp
from jax import lax
from jax.experimental import pallas as pl
from jax.experimental.pallas import tpu as pltpu
from jax.sharding import PartitionSpec as P

CREAL = 21843
UNIT = 16
MESH = pl.DeviceIdType.MESH
ANY = pl.BlockSpec(memory_space=pl.ANY)
VMEM = pl.BlockSpec(memory_space=pltpu.VMEM)


def start_of(owner, n, units):
    return lax.div(owner * units, n)


def at_width(owner, n, units, run):
    base = units // n
    wide = start_of(owner + 1, n, units) - start_of(owner, n, units) > base
    pl.when(wide)(functools.partial(run, (base + 1) * UNIT))
    pl.when(jnp.logical_not(wide))(functools.partial(run, base * UNIT))


def exchange_kernel(n, units, mean, scale, noise, out, noise_out, send, recv, nsend, nrecv, local):
    me, cls = lax.axis_index("draw"), lax.axis_index("cls")
    rows = mean.shape[1]
    barrier = pltpu.get_barrier_semaphore()
    for k in range(1, n):
        pl.semaphore_signal(barrier, inc=1, device_id=(cls, lax.rem(me + k, n)), device_id_type=MESH)
    pl.semaphore_wait(barrier, n - 1)

    def place(head, source, width):
        if rows % 128:
            return out.at[head, source, pl.ds(0, width)]
        return out.at[head, pl.ds(0, width), pl.ds(pl.multiple_of(source * rows, rows), rows)]

    def block(head, owner, width):
        start = pl.multiple_of(start_of(owner, n, units) * UNIT, UNIT)
        return (mean, scale)[head].at[pl.ds(start, width)]

    def remote(source, target, send_sem, recv_sem, device):
        return pltpu.make_async_remote_copy(
            source, target, send_sem, recv_sem, device_id=(cls, device), device_id_type=MESH
        )

    def noise_copy(slot, k, device):
        return remote(noise, noise_out.at[slot], nsend.at[k], nrecv.at[slot], device)

    def each(owner, k, source, device, act):
        for head in range(2):
            at_width(
                owner, n, units,
                lambda w: act(
                    remote(block(head, owner, w), place(head, source, w), send.at[head, k], recv.at[head, source], device)
                ),
            )

    def own(act):
        act(pltpu.make_async_copy(noise, noise_out.at[me], local.at[2]))
        for head in range(2):
            at_width(
                me, n, units,
                lambda w: act(pltpu.make_async_copy(block(head, me, w), place(head, me, w), local.at[head])),
            )

    for k in range(1, n):
        to = lax.rem(me + k, n)
        each(to, k, me, to, lambda c: c.start())
        noise_copy(me, k, to).start()
    own(lambda c: c.start())
    for k in range(1, n):
        source = lax.rem(me + n - k, n)
        each(me, k, source, source, lambda c: c.wait_recv())
        noise_copy(source, k, source).wait_recv()
    for k in range(1, n):
        to = lax.rem(me + k, n)
        each(to, k, me, to, lambda c: c.wait_send())
        noise_copy(me, k, to).wait_send()
    own(lambda c: c.wait())


def gather_kernel(n, units, cot, out, send, recv, local):
    me, cls = lax.axis_index("draw"), lax.axis_index("cls")
    half = n // 2
    group, side = lax.div(me, 2), lax.rem(me, 2)
    partner = group * 2 + 1 - side
    split = units // n // 2 * UNIT
    pieces = [(head, part) for head in range(2) for part in range(2)]
    barrier = pltpu.get_barrier_semaphore()
    peers = [partner] + [lax.rem(group + k, half) * 2 + side for k in range(1, half)]
    for peer in peers:
        pl.semaphore_signal(barrier, inc=1, device_id=(cls, peer), device_id_type=MESH)
    pl.semaphore_wait(barrier, half)

    def source(piece, width):
        head, part = pieces[piece]
        return cot.at[head, pl.ds(split, width - split) if part else pl.ds(0, split)]

    def place(piece, owner, width):
        head, part = pieces[piece]
        start = start_of(owner, n, units) * UNIT + part * split
        return out.at[head, pl.ds(pl.multiple_of(start, UNIT), width - split if part else split)]

    def send_own(piece, owner, slot, device, act):
        at_width(
            owner, n, units,
            lambda w: act(
                pltpu.make_async_remote_copy(
                    source(piece, w), place(piece, owner, w), send.at[slot, piece], recv.at[owner, piece],
                    device_id=(cls, device), device_id_type=MESH,
                )
            ),
        )

    def forward(piece, owner, slot, act):
        at_width(
            owner, n, units,
            lambda w: act(
                pltpu.make_async_remote_copy(
                    place(piece, owner, w), place(piece, owner, w), send.at[slot, piece], recv.at[owner, piece],
                    device_id=(cls, partner), device_id_type=MESH,
                )
            ),
        )

    def own(piece, act):
        at_width(
            me, n, units,
            lambda w: act(pltpu.make_async_copy(source(piece, w), place(piece, me, w), local.at[piece])),
        )

    count = len(pieces)
    for piece in range(count):
        for k in range(1, half):
            send_own(piece, me, k, peers[k], lambda c: c.start())
        send_own(piece, me, 0, partner, lambda c: c.start())
    for piece in range(count):
        own(piece, lambda c: c.start())
    order = sorted(range(1, half), key=lambda k: min(k, half - k))
    for piece in range(count):
        for k in order:
            send_own(piece, peers[k], k, peers[k], lambda c: c.wait_recv())
            forward(piece, peers[k], half + k, lambda c: c.start())
    for piece in range(count):
        send_own(piece, partner, 0, partner, lambda c: c.wait_recv())
        for k in range(1, half):
            owner = lax.rem(group + k, half) * 2 + 1 - side
            forward(piece, owner, half + k, lambda c: c.wait_recv())
    for piece in range(count):
        for k in range(half):
            send_own(piece, me, k, peers[k], lambda c: c.wait_send())
        for k in range(1, half):
            forward(piece, peers[k], half + k, lambda c: c.wait_send())
        own(piece, lambda c: c.wait())


def merge(slots, count, softmax):
    if not softmax:
        total = slots[0]
        for i in range(1, count):
            total = total + slots[i]
        return total
    top = slots[0, 0]
    for i in range(1, count):
        top = jnp.maximum(top, slots[i, 0])
    total = jnp.zeros_like(top)
    for i in range(count):
        total = total + slots[i, 1] * jnp.exp(slots[i, 0] - top)
    return jnp.stack((top, total))


def reduce_kernel(counts, softmax, x, out, *scratch):
    levels = len(counts)
    slots, sends, recvs = scratch[:levels], scratch[levels : 2 * levels], scratch[2 * levels :]
    cls, draw = lax.axis_index("cls"), lax.axis_index("draw")

    def device(level, index):
        return (index, draw) if level == 0 else (cls, index)

    barrier = pltpu.get_barrier_semaphore()
    for level, n in enumerate(counts):
        me = (cls, draw)[level]
        for k in range(1, n):
            pl.semaphore_signal(
                barrier, inc=1, device_id=device(level, lax.rem(me + k, n)), device_id_type=MESH
            )
    pl.semaphore_wait(barrier, sum(counts) - levels)
    value = x[...]
    for level, n in enumerate(counts):
        me = (cls, draw)[level]
        held = slots[level]
        held[me] = value

        def copy(slot, k, target):
            return pltpu.make_async_remote_copy(
                held.at[slot], held.at[slot], sends[level].at[k], recvs[level].at[slot],
                device_id=device(level, target), device_id_type=MESH,
            )

        for k in range(1, n):
            copy(me, k, lax.rem(me + k, n)).start()
        for k in range(1, n):
            source = lax.rem(me + n - k, n)
            copy(source, k, source).wait_recv()
        for k in range(1, n):
            copy(me, k, lax.rem(me + k, n)).wait_send()
        value = merge(held, n, softmax)
    if softmax:
        out[...] = value[0] + jnp.log(value[1])
    else:
        out[...] = value


def params(collective_id):
    return pltpu.CompilerParams(
        collective_id=collective_id, has_side_effects=True, vmem_limit_bytes=32 * 2**20
    )


def reduce_over(x, counts, softmax, collective_id):
    shape = x.shape[1:] if softmax else x.shape
    return pl.pallas_call(
        functools.partial(reduce_kernel, counts, softmax),
        out_shape=jax.ShapeDtypeStruct(shape, jnp.float32),
        in_specs=[VMEM],
        out_specs=VMEM,
        scratch_shapes=[pltpu.VMEM((n,) + x.shape, jnp.float32) for n in counts]
        + [pltpu.SemaphoreType.DMA((n,)) for n in counts]
        + [pltpu.SemaphoreType.DMA((n,)) for n in counts],
        compiler_params=params(collective_id),
    )(x)


def on_device(features, mean_head, scale_head, factor, noise, labels):
    rows, columns = mean_head.shape
    batch = features.shape[0]
    n, ncls = lax.axis_size("draw"), lax.axis_size("cls")
    me = lax.axis_index("draw")
    units = columns // UNIT
    tile = -(-units // n) * UNIT
    own, rank = noise.shape[0], noise.shape[2]
    draws = own * n
    mean_rows, scale_rows = mean_head.T, scale_head.T
    held = (2, tile, n * rows) if rows % 128 == 0 else (2, n, tile, rows)

    heads, noise_t = pl.pallas_call(
        functools.partial(exchange_kernel, n, units),
        out_shape=(
            jax.ShapeDtypeStruct(held, jnp.bfloat16),
            jax.ShapeDtypeStruct((n, own, rank, batch), jnp.bfloat16),
        ),
        in_specs=[ANY] * 3,
        out_specs=(ANY, ANY),
        scratch_shapes=[
            pltpu.SemaphoreType.DMA((2, n)),
            pltpu.SemaphoreType.DMA((2, n)),
            pltpu.SemaphoreType.DMA((n,)),
            pltpu.SemaphoreType.DMA((n,)),
            pltpu.SemaphoreType.DMA((3,)),
        ],
        compiler_params=params(0),
    )(mean_rows, scale_rows, noise.transpose(0, 2, 1))
    if rows % 128:
        heads = heads.transpose(0, 2, 1, 3).reshape(2, tile, n * rows)

    first = start_of(me, n, units) * UNIT
    width = start_of(me + 1, n, units) * UNIT - first
    offsets = jnp.arange(tile, dtype=jnp.int32)[:, None]
    valid = offsets < width
    class_ids = lax.axis_index("cls") * columns + first + offsets
    shift = jnp.where(class_ids >= CREAL, 30000.0, 0.0).astype(jnp.float32)
    my_factor = lax.dynamic_slice_in_dim(factor.T, first, tile, 1)
    my_labels = jnp.where(valid, lax.dynamic_slice_in_dim(labels.T, first, tile, 0), 0.0)

    last_dims = (((1,), (1,)), ((), ()))
    mean_logit = lax.dot_general(heads[0], features, last_dims, preferred_element_type=jnp.float32)
    scale_pre = lax.dot_general(heads[1], features, last_dims, preferred_element_type=jnp.float32)
    scale_pre = jnp.where(valid, scale_pre, 0.0)
    spread = jax.nn.softplus(scale_pre)
    lowrank = jnp.einsum(
        "rc,srb->scb", my_factor, noise_t.reshape(draws, rank, batch), preferred_element_type=jnp.float32
    )
    logits = mean_logit[None] + spread[None] * lowrank - shift[None]
    logits = jnp.where(valid[None], logits, -1e30)
    local_top = jnp.max(logits, axis=1)
    local_total = jnp.sum(jnp.exp(logits - local_top[:, None]), axis=1)
    lse = reduce_over(jnp.stack((local_top, local_total)), (ncls, n), True, 1)
    log_prob = logits - lse[:, None]
    best = jnp.max(log_prob, axis=0)
    mix = best + jnp.log(jnp.sum(jnp.exp(log_prob - best[None]), axis=0))
    ratio = jnp.exp(log_prob - mix[None])
    label_dot = reduce_over(jnp.sum(my_labels[None] * ratio, axis=1), (ncls, n), False, 2)
    logit_cot = (jnp.exp(log_prob) * label_dot[:, None] - my_labels[None] * ratio) / batch
    dmean = jnp.sum(logit_cot, axis=0)
    dspread = jnp.sum(logit_cot * lowrank, axis=0)
    cots = jnp.stack((dmean, dspread * jax.nn.sigmoid(scale_pre))).astype(jnp.bfloat16)

    gathered = pl.pallas_call(
        functools.partial(gather_kernel, n, units),
        out_shape=jax.ShapeDtypeStruct((2, columns, batch), jnp.bfloat16),
        in_specs=[ANY],
        out_specs=ANY,
        scratch_shapes=[
            pltpu.SemaphoreType.DMA((n, 4)),
            pltpu.SemaphoreType.DMA((n, 4)),
            pltpu.SemaphoreType.DMA((4,)),
        ],
        compiler_params=params(3),
    )(cots)
    mean_cot, scale_cot = gathered[0], gathered[1]
    my_columns = lax.dynamic_slice_in_dim(features, me * rows, rows, 1)
    over_classes = (((0,), (0,)), ((), ()))
    feature_part = lax.dot_general(
        mean_cot, mean_rows, over_classes, preferred_element_type=jnp.float32
    ) + lax.dot_general(scale_cot, scale_rows, over_classes, preferred_element_type=jnp.float32)
    mean_grad = jnp.dot(mean_cot, my_columns, preferred_element_type=jnp.float32).T
    scale_grad = jnp.dot(scale_cot, my_columns, preferred_element_type=jnp.float32).T
    feature_grad, step = feature_part, 1
    while step < ncls:
        feature_grad = feature_grad + lax.ppermute(feature_grad, "cls", [(i, i ^ step) for i in range(ncls)])
        step *= 2
    return (mean_grad, scale_grad, feature_grad)


def solution(mesh):
    return jax.shard_map(
        on_device,
        mesh=mesh,
        in_specs=(
            P(),
            P("draw", "cls"),
            P("draw", "cls"),
            P("cls", None),
            P("draw", None, None),
            P(None, "cls"),
        ),
        out_specs=(P("draw", "cls"), P("draw", "cls"), P(None, "draw")),
        check_vma=False,
    )
```

time: 196 us -> 168 us (0.86)
  Pallas kernels: 164 us -> 135 us
  local copies, waits for them, and re-layouts: 7.59 us -> 3.52 us
  starting transfers between devices: 0 us -> 3.34 us
  matrix products: 8.42 us -> 11.3 us
    pallas_call x2, Pallas kernels: 139 us -> 113 us  [the longest x1 68 us: on_device(): pl.pallas_call(functools.partial(exchange_kernel, n, units), out_shape=(j...]
    pallas_call x3 -> x2, Pallas kernels: 25.9 us -> 21.8 us  [reduce_over(): pl.pallas_call(functools.partial(reduce_kernel, counts, softmax), out_sha...]
    ppermute x0 -> x2, starting transfers between devices: none -> 3.34 us  [on_device(): lax.ppermute(feature_grad, 'cls', [(i, i ^ step) for i in range(ncls)])]
    dot_general x7, matrix products: 8.42 us -> 11.3 us  [the longest x1 2.82 us: on_device(): jnp.dot(scale_cot, my_columns, preferred_element_type=jnp.float32)]
    dynamic_slice x2 -> x0, local copies, waits for them, and re-layouts: 2.01 us -> none  [on_device(): my_labels = lax.dynamic_slice_in_dim(widen(labels), first, tile, 1)]
    unnamed x14 -> x11, local copies, waits for them, and re-layouts: 5.11 us -> 3.52 us
  transfers between devices with their start and end apart: 0 -> 2, of which waited for: 0 -> 0; matrix products, arithmetic and copies ran while one was open for 0% -> 3% of each run, Pallas kernels for 0% -> 0%
where the time goes in v2:
time: 168 us; the launch traced here: 167 us
  Pallas kernels  135 us (80%)
  other arithmetic  13.7 us (8%)
  matrix products  11.3 us (7%)
  local copies, waits for them, and re-layouts  3.52 us (2%)
  starting transfers between devices  3.34 us (2%)
    pallas_call x1, Pallas kernels, on_device(): pl.pallas_call(functools.partial(exchange_kernel, n, units), out_shape=(j...  68 us
    pallas_call x1, Pallas kernels, on_device(): pl.pallas_call(functools.partial(gather_kernel, n, units), out_shape=jax....  44.6 us
    pallas_call x2, Pallas kernels, reduce_over(): pl.pallas_call(functools.partial(reduce_kernel, counts, softmax), out_sha...  21.8 us
    reduce_sum x1, other arithmetic, on_device(): dmean = jnp.sum(logit_cot, axis=0)  3.78 us
    unnamed x11, local copies, waits for them, and re-layouts  3.52 us
  transfers between devices with their start and end apart: 2, of which 0 were waited for; matrix products, arithmetic and copies ran while one was open for 3% of the time, Pallas kernels for 0%

profile of v2, /device:TPU:9, one launch (start us, length us, event | category | flops | bytes accessed | tf_op | source)
XLA Modules:
  0.0 167.3 jit_solution(15128309682881505015)
XLA Ops:
  0.7 0.8 copy.11
  1.5 1.3 copy-done.1
  2.8 1.3 copy-done.3
  4.2 68.0 %shard_map.85 = (bf16[2,688,1024]{2,1,0:T(8,128)(2,1)S(1)}, bf16[8,2,50,128]{3,2,1,0:T(8,128)(2,1)S(1)}) custom-call(bf16[5472,128]{1,0:T(8,128)(2,1)S(1)} %bitcast.73, bf16[5472,128]{1,0:T(8,128)(2,1)S(1)} %bitcast.72, bf16[2,50,128]{2,1,0:T(8,128)(2,1)S(1)} %bitcast.74), custom_call_target="tpu_custom_call" | custom-call | tf_op jit(solution)/shard_map/pallas_call | solution.py:249
  72.2 1.5 fusion.8
  73.7 1.6 compare_select_fusion
  75.3 1.5 fusion.40
  76.9 1.8 %exponential_reduce_fusion.1 = f32[16,128]{1,0:T(8,128)S(1)} fusion(f32[16,128]{1,0:T(8,128)S(1)} %get-tuple-element.11, f32[688]{0:T(1024)S(1)} %fusion.36, f32[16,128,688]{1,2,0:T(8,128)S(1)} %get-tuple-element.12, f32[688,128]{1,0:T(8,128)S(1)} %get-tuple-element.9, f32[688,128]{1,0:T(8,128)S(1)} %fusion.8, pred[688]{0:T(1024)(128)(4,1)S(1)} %iota_compare_fusion), kind=kLoop, calls=%fused_computation.9 | loop fusion | flops 8452096 | bytes 6360432 | tf_op jit(solution)/shard_map/reduce_sum | solution.py:289
  78.7 13.0 %shard_map.86 = f32[16,128]{1,0:T(8,128)S(1)} custom-call(f32[2,16,128]{2,1,0:T(8,128)S(1)} %pad_maximum_fusion.1.x), custom_call_target="tpu_custom_call" | custom-call | tf_op jit(solution)/shard_map/pallas_call | solution.py:225
  91.7 1.6 subtract_reduce_fusion
  93.3 2.2 %exponential_reduce_fusion = f32[688,128]{1,0:T(8,128)S(1)} fusion(f32[688,128]{1,0:T(8,128)S(1)} %subtract_reduce_fusion, f32[16,128]{1,0:T(8,128)S(1)} %shard_map.86, f32[688]{0:T(1024)S(1)} %fusion.36, f32[16,128,688]{1,2,0:T(8,128)S(1)} %get-tuple-element.12, f32[688,128]{1,0:T(8,128)S(1)} %get-tuple-element.9, f32[688,128]{1,0:T(8,128)S(1)} %fusion.8, ...), kind=kLoop, calls=%fused_computation.8 | loop fusion | flops 9775104 | bytes 7056752 | tf_op jit(solution)/shard_map/reduce_sum | solution.py:293
  95.6 1.1 select_bitcast_fusion
  96.8 2.2 %fusion.4.x = f32[16,128]{1,0:T(8,128)S(1)} fusion(f32[688,128]{1,0:T(8,128)S(1)} %log_add_fusion, f32[688,128]{1,0:T(8,128)S(1)} %select_bitcast_fusion, f32[16,128]{1,0:T(8,128)S(1)} %shard_map.86, f32[688]{0:T(1024)S(1)} %fusion.36, f32[16,128,688]{1,2,0:T(8,128)S(1)} %get-tuple-element.12, f32[688,128]{1,0:T(8,128)S(1)} %get-tuple-element.9, ...), kind=kLoop, calls=%fused_computation.10 | loop fusion | flops 11270144 | bytes 7064944 | tf_op jit(solution)/shard_map/reduce_sum | solution.py:295
  99.0 8.9 %shard_map.87 = f32[16,128]{1,0:T(8,128)S(1)} custom-call(f32[16,128]{1,0:T(8,128)S(1)} %fusion.4.x), custom_call_target="tpu_custom_call" | custom-call | tf_op jit(solution)/shard_map/pallas_call | solution.py:225
  107.9 3.8 %fusion.5 = (bf16[688,128]{1,0:T(8,128)(2,1)S(1)}, f32[688,128]{1,0:T(8,128)S(1)}) fusion(f32[16,128]{1,0:T(8,128)S(1)} %shard_map.87, f32[688,128]{1,0:T(8,128)S(1)} %log_add_fusion, f32[688,128]{1,0:T(8,128)S(1)} %select_bitcast_fusion, f32[16,128]{1,0:T(8,128)S(1)} %shard_map.86, f32[688]{0:T(1024)S(1)} %fusion.36, ...), kind=kLoop, calls=%fused_computation.12 | loop fusion | flops 18141184 | bytes 7593328 | tf_op jit(solution)/shard_map/reduce_sum | solution.py:297
  111.7 0.1 fusion.30
  111.8 44.6 %shard_map.88 = bf16[2,5472,128]{2,1,0:T(8,128)(2,1)S(1)} custom-call(bf16[2,688,128]{2,1,0:T(8,128)(2,1)S(1)} %pad_maximum_fusion.cot), custom_call_target="tpu_custom_call" | custom-call | tf_op jit(solution)/shard_map/pallas_call | solution.py:301
  156.5 0.6 fusion.12
  157.1 0.6 fusion.27
  157.6 2.1 %collective-permute-start = (f32[128,128]{1,0:T(8,128)S(1)}, f32[128,128]{1,0:T(8,128)S(1)}, u32[]{:S(2)}, u32[]{:S(2)}) collective-permute-start(f32[128,128]{1,0:T(8,128)S(1)} %fusion.27), channel_id=1, source_target_pairs={{0,8},{8,0},{16,24},{24,16},{1,9},{9,1},{17,25},{25,17},{2,10},{10... | collective-permute-start | bytes 196616 | tf_op jit(solution)/shard_map/ppermute | solution.py:323
  159.7 2.8 %fusion.18 = f32[128,5472]{0,1:T(8,128)} fusion(bf16[2,5472,128]{2,1,0:T(8,128)(2,1)S(1)} %shard_map.88, bf16[128,1024]{1,0:T(8,128)(2,1)} %param.6, s32[]{:T(128)S(6)} %select_n.35), kind=kOutput, calls=%fused_computation.25 | convolution fusion | flops 179306496 | bytes 4235268 | tf_op jit(solution)/shard_map/dot_general | solution.py:319
  162.5 1.3 collective-permute-start.1
  163.8 2.8 %fusion.14 = f32[128,5472]{0,1:T(8,128)} fusion(bf16[2,5472,128]{2,1,0:T(8,128)(2,1)S(1)} %shard_map.88, bf16[128,1024]{1,0:T(8,128)(2,1)} %param.6, s32[]{:T(128)S(6)} %select_n.35), kind=kOutput, calls=%fused_computation.21 | convolution fusion | flops 179306496 | bytes 4235268 | tf_op jit(solution)/shard_map/dot_general | solution.py:320
  166.6 0.6 add.69
  (16 shorter events, 0.2 us)
Async XLA Ops:
  0.6 74.7 %copy-start = (bf16[5472,50]{0,1:T(8,128)(2,1)S(1)}, bf16[5472,50]{0,1:T(8,128)(2,1)}, u32[]{:S(2)}) copy-start(bf16[5472,50]{0,1:T(8,128)(2,1)} %param.9) | copy-start | bytes 1641604
  1.5 1.4 copy-start.1
  2.8 1.3 copy-start.3
  107.9 48.6 %copy-start.2 = (bf16[128,5472]{0,1:T(8,128)(2,1)S(1)}, bf16[128,5472]{0,1:T(8,128)(2,1)}, u32[]{:S(2)}) copy-start(bf16[128,5472]{0,1:T(8,128)(2,1)} %param.8) | copy-start | bytes 4202500
  111.7 45.4 %copy-start.4 = (bf16[128,5472]{0,1:T(8,128)(2,1)S(1)}, bf16[128,5472]{0,1:T(8,128)(2,1)}, u32[]{:S(2)}) copy-start(bf16[128,5472]{0,1:T(8,128)(2,1)} %param.7) | copy-start | bytes 4202500
  157.6 4.9 %collective-permute-start = (f32[128,128]{1,0:T(8,128)S(1)}, f32[128,128]{1,0:T(8,128)S(1)}, u32[]{:S(2)}, u32[]{:S(2)}) collective-permute-start(f32[128,128]{1,0:T(8,128)S(1)} %fusion.27), channel_id=1, source_target_pairs={{0,8},{8,0},{16,24},{24,16},{1,9},{9,1},{17,25},{25,17},{2,10},{10... | collective-permute-start | bytes 196616 | tf_op jit(solution)/shard_map/ppermute | solution.py:323
  162.5 4.1 %collective-permute-start.1 = (f32[128,128]{1,0:T(8,128)S(1)}, f32[128,128]{1,0:T(8,128)S(1)}, u32[]{:S(2)}, u32[]{:S(2)}) collective-permute-start(f32[128,128]{1,0:T(8,128)S(1)} %add.68), channel_id=1, source_target_pairs={{0,16},{8,24},{16,0},{24,8},{1,17},{9,25},{17,1},{25,9},{2,18},{10... | collective-permute-start | bytes 196616 | tf_op jit(solution)/shard_map/ppermute | solution.py:323

commit v3 on v2

--- a/solution.py
+++ b/solution.py
@@ -24,62 +24,103 @@
     pl.when(jnp.logical_not(wide))(functools.partial(run, base * UNIT))
 
 
-def exchange_kernel(n, units, mean, scale, noise, out, noise_out, send, recv, nsend, nrecv, local):
+def exchange_kernel(
+    n, units, feat, mean, scale, noise, logits, noise_out, held, part_out, part_in,
+    send, recv, part_send, part_recv, nsend, nrecv, local, nlocal,
+):
     me, cls = lax.axis_index("draw"), lax.axis_index("cls")
-    rows = mean.shape[1]
+    half = n // 2
+    mirror = lax.rem(me + half, n)
+    base, spot = lax.div(me, half) * half, lax.rem(me, half)
     barrier = pltpu.get_barrier_semaphore()
     for k in range(1, n):
         pl.semaphore_signal(barrier, inc=1, device_id=(cls, lax.rem(me + k, n)), device_id_type=MESH)
     pl.semaphore_wait(barrier, n - 1)
 
-    def place(head, source, width):
-        if rows % 128:
-            return out.at[head, source, pl.ds(0, width)]
-        return out.at[head, pl.ds(0, width), pl.ds(pl.multiple_of(source * rows, rows), rows)]
+    def remote(source, target, send_sem, recv_sem, device):
+        return pltpu.make_async_remote_copy(
+            source, target, send_sem, recv_sem, device_id=(cls, device), device_id_type=MESH
+        )
+
+    def noise_copy(slot, k, device):
+        return remote(noise, noise_out.at[slot], nsend.at[k], nrecv.at[slot], device)
 
     def block(head, owner, width):
         start = pl.multiple_of(start_of(owner, n, units) * UNIT, UNIT)
         return (mean, scale)[head].at[pl.ds(start, width)]
 
-    def remote(source, target, send_sem, recv_sem, device):
-        return pltpu.make_async_remote_copy(
-            source, target, send_sem, recv_sem, device_id=(cls, device), device_id_type=MESH
-        )
-
-    def noise_copy(slot, k, device):
-        return remote(noise, noise_out.at[slot], nsend.at[k], nrecv.at[slot], device)
-
-    def each(owner, k, source, device, act):
-        for head in range(2):
-            at_width(
-                owner, n, units,
-                lambda w: act(
-                    remote(block(head, owner, w), place(head, source, w), send.at[head, k], recv.at[head, source], device)
-                ),
+    def block_copy(far, head, owner, k, source, device, act):
+        at_width(
+            owner, n, units,
+            lambda w: act(
+                remote(
+                    block(head, owner, w), held.at[far, head, source, pl.ds(0, w)],
+                    send.at[far, head, k], recv.at[far, head, source], device,
+                )
+            ),
+        )
+
+    def own_copy(far, head, act):
+        owner = mirror if far else me
+        at_width(
+            owner, n, units,
+            lambda w: act(
+                pltpu.make_async_copy(
+                    block(head, owner, w), held.at[far, head, spot, pl.ds(0, w)], local.at[far, head]
+                )
+            ),
+        )
+
+    def sends(far, head, act):
+        for k in range(1, half):
+            peer = base + lax.rem(spot + k, half)
+            block_copy(far, head, lax.rem(peer + half, n) if far else peer, k, spot, peer, act)
+
+    def arrive(far, head):
+        owner = mirror if far else me
+        for k in range(1, half):
+            source = lax.rem(spot + half - k, half)
+            block_copy(far, head, owner, k, source, base + source, lambda c: c.wait_recv())
+        own_copy(far, head, lambda c: c.wait())
+        total = None
+        for source in range(half):
+            term = lax.dot_general(
+                held[far, head, source], feat[source], (((1,), (1,)), ((), ())), preferred_element_type=jnp.float32
             )
-
-    def own(act):
-        act(pltpu.make_async_copy(noise, noise_out.at[me], local.at[2]))
-        for head in range(2):
-            at_width(
-                me, n, units,
-                lambda w: act(pltpu.make_async_copy(block(head, me, w), place(head, me, w), local.at[head])),
-            )
-
+            total = term if total is None else total + term
+        return total
+
+    def part_copy(head):
+        return remote(part_out.at[head], part_in.at[head], part_send.at[head], part_recv.at[head], mirror)
+
+    own_noise = pltpu.make_async_copy(noise, noise_out.at[me], nlocal)
+    stages = [(1, 0), (1, 1), (0, 0), (0, 1)]
+    sends(1, 0, lambda c: c.start())
     for k in range(1, n):
-        to = lax.rem(me + k, n)
-        each(to, k, me, to, lambda c: c.start())
-        noise_copy(me, k, to).start()
-    own(lambda c: c.start())
+        noise_copy(me, k, lax.rem(me + k, n)).start()
+    for far, head in stages[1:]:
+        sends(far, head, lambda c: c.start())
+    for far, head in stages:
+        own_copy(far, head, lambda c: c.start())
+    own_noise.start()
+    for head in range(2):
+        part_out[head] = arrive(1, head)
+        part_copy(head).start()
+    for head in range(2):
+        logits[head] = arrive(0, head)
     for k in range(1, n):
         source = lax.rem(me + n - k, n)
-        each(me, k, source, source, lambda c: c.wait_recv())
         noise_copy(source, k, source).wait_recv()
+    own_noise.wait()
+    for head in range(2):
+        part_copy(head).wait_recv()
+        logits[head] = logits[head] + part_in[head]
+    for far, head in stages:
+        sends(far, head, lambda c: c.wait_send())
     for k in range(1, n):
-        to = lax.rem(me + k, n)
-        each(to, k, me, to, lambda c: c.wait_send())
-        noise_copy(me, k, to).wait_send()
-    own(lambda c: c.wait())
+        noise_copy(me, k, lax.rem(me + k, n)).wait_send()
+    for head in range(2):
+        part_copy(head).wait_send()
 
 
 def gather_kernel(n, units, cot, out, send, recv, local):
@@ -244,27 +285,33 @@
     own, rank = noise.shape[0], noise.shape[2]
     draws = own * n
     mean_rows, scale_rows = mean_head.T, scale_head.T
-    held = (2, tile, n * rows) if rows % 128 == 0 else (2, n, tile, rows)
+    half = n // 2
+    my_half = lax.dynamic_slice_in_dim(features, lax.div(me, half) * (half * rows), half * rows, 1)
+    feat = my_half.reshape(batch, half, rows).transpose(1, 0, 2)
 
     heads, noise_t = pl.pallas_call(
         functools.partial(exchange_kernel, n, units),
         out_shape=(
-            jax.ShapeDtypeStruct(held, jnp.bfloat16),
+            jax.ShapeDtypeStruct((2, tile, batch), jnp.float32),
             jax.ShapeDtypeStruct((n, own, rank, batch), jnp.bfloat16),
         ),
-        in_specs=[ANY] * 3,
-        out_specs=(ANY, ANY),
+        in_specs=[VMEM] + [ANY] * 3,
+        out_specs=(VMEM, ANY),
         scratch_shapes=[
-            pltpu.SemaphoreType.DMA((2, n)),
-            pltpu.SemaphoreType.DMA((2, n)),
+            pltpu.VMEM((2, 2, half, tile, rows), jnp.bfloat16),
+            pltpu.VMEM((2, tile, batch), jnp.float32),
+            pltpu.VMEM((2, tile, batch), jnp.float32),
+            pltpu.SemaphoreType.DMA((2, 2, half)),
+            pltpu.SemaphoreType.DMA((2, 2, half)),
+            pltpu.SemaphoreType.DMA((2,)),
+            pltpu.SemaphoreType.DMA((2,)),
             pltpu.SemaphoreType.DMA((n,)),
             pltpu.SemaphoreType.DMA((n,)),
-            pltpu.SemaphoreType.DMA((3,)),
+            pltpu.SemaphoreType.DMA((2, 2)),
+            pltpu.SemaphoreType.DMA,
         ],
         compiler_params=params(0),
-    )(mean_rows, scale_rows, noise.transpose(0, 2, 1))
-    if rows % 128:
-        heads = heads.transpose(0, 2, 1, 3).reshape(2, tile, n * rows)
+    )(feat, mean_rows, scale_rows, noise.transpose(0, 2, 1))
 
     first = start_of(me, n, units) * UNIT
     width = start_of(me + 1, n, units) * UNIT - first
@@ -275,9 +322,7 @@
     my_factor = lax.dynamic_slice_in_dim(factor.T, first, tile, 1)
     my_labels = jnp.where(valid, lax.dynamic_slice_in_dim(labels.T, first, tile, 0), 0.0)
 
-    last_dims = (((1,), (1,)), ((), ()))
-    mean_logit = lax.dot_general(heads[0], features, last_dims, preferred_element_type=jnp.float32)
-    scale_pre = lax.dot_general(heads[1], features, last_dims, preferred_element_type=jnp.float32)
+    mean_logit, scale_pre = heads[0], heads[1]
     scale_pre = jnp.where(valid, scale_pre, 0.0)
     spread = jax.nn.softplus(scale_pre)
     lowrank = jnp.einsum(

time: 168 us -> 149 us (0.89)
  Pallas kernels: 135 us -> 118 us
  matrix products: 11.3 us -> 8.29 us
    pallas_call x1, Pallas kernels: 68 us -> 52.9 us  [on_device(): pl.pallas_call(functools.partial(exchange_kernel, n, units), out_shape=(j...]
    dot_general x2 -> x0, matrix products: 3.04 us -> none  [the longest x1 1.56 us: on_device(): lax.dot_general(heads[1], features, last_dims, preferred_element_type=jnp...]
    unnamed x11 -> x12, local copies, waits for them, and re-layouts: 3.52 us -> 3.59 us
  transfers between devices with their start and end apart: 2 -> 2, of which waited for: 0 -> 0; matrix products, arithmetic and copies ran while one was open for 3% -> 4% of each run, Pallas kernels for 0% -> 0%
where the time goes in v3:
time: 149 us
  Pallas kernels  118 us (79%)
  other arithmetic  14 us (9%)
  matrix products  8.29 us (6%)
  local copies, waits for them, and re-layouts  4.7 us (3%)
  starting transfers between devices  3.09 us (2%)
    pallas_call x1, Pallas kernels, on_device(): pl.pallas_call(functools.partial(exchange_kernel, n, units), out_shape=(j...  52.9 us
    pallas_call x1, Pallas kernels, on_device(): pl.pallas_call(functools.partial(gather_kernel, n, units), out_shape=jax....  43.8 us
    pallas_call x2, Pallas kernels, reduce_over(): pl.pallas_call(functools.partial(reduce_kernel, counts, softmax), out_sha...  21 us
    reduce_sum x1, other arithmetic, on_device(): dmean = jnp.sum(logit_cot, axis=0)  3.78 us
    unnamed x12, local copies, waits for them, and re-layouts  3.59 us
    ppermute x2, starting transfers between devices, on_device(): lax.ppermute(feature_grad, 'cls', [(i, i ^ step) for i in range(ncls)])  3.09 us
  transfers between devices with their start and end apart: 2, of which 0 were waited for; matrix products, arithmetic and copies ran while one was open for 4% of the time, Pallas kernels for 0%

profile of v3, /device:TPU:9, one launch (start us, length us, event | category | flops | bytes accessed | tf_op | source)
XLA Modules:
  0.0 148.8 jit_solution(3560986981312464354)
XLA Ops:
  0.7 1.0 constant_dynamic-slice_fusion
  1.9 0.8 copy.15
  2.7 1.3 copy-done.1
  4.0 1.3 copy-done.3
  5.4 52.9 %shard_map.85 = (f32[2,688,128]{2,1,0:T(8,128)S(1)}, bf16[8,2,50,128]{3,2,1,0:T(8,128)(2,1)S(1)}) custom-call(bf16[4,128,128]{2,1,0:T(8,128)(2,1)S(1)} %bitcast.70, bf16[5472,128]{1,0:T(8,128)(2,1)S(1)} %bitcast.69, bf16[5472,128]{1,0:T(8,128)(2,1)S(1)} %bitcast.68, bf16[2,50,128]{2,1,0:T(8,128)(2,1)S(1)} %bitcast.71), custom_call_target="tpu_custom_call" | custom-call | tf_op jit(solution)/shard_map/pallas_call | solution.py:292
  58.3 0.3 slice_bitcast_fusion
  58.7 1.5 %fusion.32 = (f32[16,128]{1,0:T(8,128)S(1)}, f32[16,128,688]{1,2,0:T(8,128)S(1)}) fusion(f32[688]{0:T(1024)S(1)} %fusion.28, f32[688,128]{1,0:T(8,128)S(1)} %get-tuple-element.10, f32[688,128]{1,0:T(8,128)S(1)} %get-tuple-element.9, pred[688]{0:T(1024)(128)(4,1)S(1)} %iota_compare_fusion, bf16[16,50,128]{2,1,0:T(8,128)(2,1)S(1)} %bitcast.72, ...), kind=kOutput, calls=%fused_computation.50 | convolution fusion | flops 147945472 | bytes 6669316 | tf_op jit(solution)/shard_map/rc,srb->scb/dot_general | solution.py:328
  60.2 1.8 %exponential_reduce_fusion.1 = f32[16,128]{1,0:T(8,128)S(1)} fusion(f32[16,128]{1,0:T(8,128)S(1)} %get-tuple-element.11, f32[688]{0:T(1024)S(1)} %fusion.28, f32[16,128,688]{1,2,0:T(8,128)S(1)} %get-tuple-element.12, f32[688,128]{1,0:T(8,128)S(1)} %get-tuple-element.10, f32[688,128]{1,0:T(8,128)S(1)} %get-tuple-element.9, pred[688]{0:T(1024)(128)(4,1)S(1)} %iota_compare_fusion), kind=kLoop, calls=%fused_computation.9 | loop fusion | flops 8452096 | bytes 6360432 | tf_op jit(solution)/shard_map/reduce_sum | solution.py:334
  62.1 11.5 %shard_map.86 = f32[16,128]{1,0:T(8,128)S(1)} custom-call(f32[2,16,128]{2,1,0:T(8,128)S(1)} %pad_maximum_fusion.1.x), custom_call_target="tpu_custom_call" | custom-call | tf_op jit(solution)/shard_map/pallas_call | solution.py:266
  73.5 1.6 %subtract_reduce_fusion = f32[688,128]{1,0:T(8,128)S(1)} fusion(f32[16,128]{1,0:T(8,128)S(1)} %shard_map.86, f32[688]{0:T(1024)S(1)} %fusion.28, f32[16,128,688]{1,2,0:T(8,128)S(1)} %get-tuple-element.12, f32[688,128]{1,0:T(8,128)S(1)} %get-tuple-element.10, f32[688,128]{1,0:T(8,128)S(1)} %get-tuple-element.9, pred[688]{0:T(1024)(128)(4,1)S(1)} %iota_compare_fusion), kind=kLoop, calls=%fused_computation.11 | loop fusion | flops 8366080 | bytes 6704496 | tf_op jit(solution)/shard_map/reduce_max | solution.py:337
  75.1 2.2 %exponential_reduce_fusion = f32[688,128]{1,0:T(8,128)S(1)} fusion(f32[688,128]{1,0:T(8,128)S(1)} %subtract_reduce_fusion, f32[16,128]{1,0:T(8,128)S(1)} %shard_map.86, f32[688]{0:T(1024)S(1)} %fusion.28, f32[16,128,688]{1,2,0:T(8,128)S(1)} %get-tuple-element.12, f32[688,128]{1,0:T(8,128)S(1)} %get-tuple-element.10, f32[688,128]{1,0:T(8,128)S(1)} %get-tuple-element.9, ...), kind=kLoop, calls=%fused_computation.8 | loop fusion | flops 9775104 | bytes 7056752 | tf_op jit(solution)/shard_map/reduce_sum | solution.py:338
  77.4 1.1 select_bitcast_fusion
  78.6 2.2 %fusion.4.x = f32[16,128]{1,0:T(8,128)S(1)} fusion(f32[688,128]{1,0:T(8,128)S(1)} %log_add_fusion, f32[688,128]{1,0:T(8,128)S(1)} %select_bitcast_fusion, f32[16,128]{1,0:T(8,128)S(1)} %shard_map.86, f32[688]{0:T(1024)S(1)} %fusion.28, f32[16,128,688]{1,2,0:T(8,128)S(1)} %get-tuple-element.12, f32[688,128]{1,0:T(8,128)S(1)} %get-tuple-element.10, ...), kind=kLoop, calls=%fused_computation.10 | loop fusion | flops 11270144 | bytes 7064944 | tf_op jit(solution)/shard_map/reduce_sum | solution.py:340
  80.8 9.6 %shard_map.87 = f32[16,128]{1,0:T(8,128)S(1)} custom-call(f32[16,128]{1,0:T(8,128)S(1)} %fusion.4.x), custom_call_target="tpu_custom_call" | custom-call | tf_op jit(solution)/shard_map/pallas_call | solution.py:266
  90.4 3.8 %fusion.5 = (bf16[688,128]{1,0:T(8,128)(2,1)S(1)}, f32[688,128]{1,0:T(8,128)S(1)}) fusion(f32[16,128]{1,0:T(8,128)S(1)} %shard_map.87, f32[688,128]{1,0:T(8,128)S(1)} %log_add_fusion, f32[688,128]{1,0:T(8,128)S(1)} %select_bitcast_fusion, f32[16,128]{1,0:T(8,128)S(1)} %shard_map.86, f32[688]{0:T(1024)S(1)} %fusion.28, ...), kind=kLoop, calls=%fused_computation.12 | loop fusion | flops 18141184 | bytes 7593328 | tf_op jit(solution)/shard_map/reduce_sum | solution.py:342
  94.2 0.2 fusion.22
  94.4 43.8 %shard_map.88 = bf16[2,5472,128]{2,1,0:T(8,128)(2,1)S(1)} custom-call(bf16[2,688,128]{2,1,0:T(8,128)(2,1)S(1)} %pad_maximum_fusion.cot), custom_call_target="tpu_custom_call" | custom-call | tf_op jit(solution)/shard_map/pallas_call | solution.py:346
  138.3 0.6 fusion.6
  138.8 0.6 fusion.18
  139.4 1.8 %collective-permute-start = (f32[128,128]{1,0:T(8,128)S(1)}, f32[128,128]{1,0:T(8,128)S(1)}, u32[]{:S(2)}, u32[]{:S(2)}) collective-permute-start(f32[128,128]{1,0:T(8,128)S(1)} %fusion.18), channel_id=1, source_target_pairs={{0,8},{8,0},{16,24},{24,16},{1,9},{9,1},{17,25},{25,17},{2,10},{10... | collective-permute-start | bytes 196616 | tf_op jit(solution)/shard_map/ppermute | solution.py:368
  141.2 2.8 %fusion.12 = f32[128,5472]{0,1:T(8,128)} fusion(bf16[2,5472,128]{2,1,0:T(8,128)(2,1)S(1)} %shard_map.88, bf16[128,1024]{1,0:T(8,128)(2,1)} %param.6, s32[]{:T(128)S(6)} %select_n.41), kind=kOutput, calls=%fused_computation.19 | convolution fusion | flops 179306496 | bytes 4235268 | tf_op jit(solution)/shard_map/dot_general | solution.py:364
  144.1 1.3 collective-permute-start.1
  145.3 2.8 %fusion.8 = f32[128,5472]{0,1:T(8,128)} fusion(bf16[2,5472,128]{2,1,0:T(8,128)(2,1)S(1)} %shard_map.88, bf16[128,1024]{1,0:T(8,128)(2,1)} %param.6, s32[]{:T(128)S(6)} %select_n.41), kind=kOutput, calls=%fused_computation.15 | convolution fusion | flops 179306496 | bytes 4235268 | tf_op jit(solution)/shard_map/dot_general | solution.py:365
  148.1 0.6 add.78
  (18 shorter events, 0.4 us)
Async XLA Ops:
  0.6 58.0 %copy-start = (bf16[5472,50]{0,1:T(8,128)(2,1)S(1)}, bf16[5472,50]{0,1:T(8,128)(2,1)}, u32[]{:S(2)}) copy-start(bf16[5472,50]{0,1:T(8,128)(2,1)} %param.9) | copy-start | bytes 1641604
  2.7 1.4 copy-start.1
  4.0 1.3 copy-start.3
  90.4 47.8 %copy-start.2 = (bf16[128,5472]{0,1:T(8,128)(2,1)S(1)}, bf16[128,5472]{0,1:T(8,128)(2,1)}, u32[]{:S(2)}) copy-start(bf16[128,5472]{0,1:T(8,128)(2,1)} %param.8) | copy-start | bytes 4202500
  94.2 44.6 %copy-start.4 = (bf16[128,5472]{0,1:T(8,128)(2,1)S(1)}, bf16[128,5472]{0,1:T(8,128)(2,1)}, u32[]{:S(2)}) copy-start(bf16[128,5472]{0,1:T(8,128)(2,1)} %param.7) | copy-start | bytes 4202500
  139.4 4.6 %collective-permute-start = (f32[128,128]{1,0:T(8,128)S(1)}, f32[128,128]{1,0:T(8,128)S(1)}, u32[]{:S(2)}, u32[]{:S(2)}) collective-permute-start(f32[128,128]{1,0:T(8,128)S(1)} %fusion.18), channel_id=1, source_target_pairs={{0,8},{8,0},{16,24},{24,16},{1,9},{9,1},{17,25},{25,17},{2,10},{10... | collective-permute-start | bytes 196616 | tf_op jit(solution)/shard_map/ppermute | solution.py:368
  144.1 4.1 %collective-permute-start.1 = (f32[128,128]{1,0:T(8,128)S(1)}, f32[128,128]{1,0:T(8,128)S(1)}, u32[]{:S(2)}, u32[]{:S(2)}) collective-permute-start(f32[128,128]{1,0:T(8,128)S(1)} %add.77), channel_id=1, source_target_pairs={{0,16},{8,24},{16,0},{24,8},{1,17},{9,25},{17,1},{25,9},{2,18},{10... | collective-permute-start | bytes 196616 | tf_op jit(solution)/shard_map/ppermute | solution.py:368

commit v4 on v3

--- a/solution.py
+++ b/solution.py
@@ -29,7 +29,7 @@
     send, recv, part_send, part_recv, nsend, nrecv, local, nlocal,
 ):
     me, cls = lax.axis_index("draw"), lax.axis_index("cls")
-    half = n // 2
+    half, rows = n // 2, mean.shape[1]
     mirror = lax.rem(me + half, n)
     base, spot = lax.div(me, half) * half, lax.rem(me, half)
     barrier = pltpu.get_barrier_semaphore()
@@ -76,6 +76,11 @@
             peer = base + lax.rem(spot + k, half)
             block_copy(far, head, lax.rem(peer + half, n) if far else peer, k, spot, peer, act)
 
+    def columns_of(source):
+        if rows % 128:
+            return feat[source]
+        return feat[:, pl.ds(pl.multiple_of(source * rows, rows), rows)]
+
     def arrive(far, head):
         owner = mirror if far else me
         for k in range(1, half):
@@ -85,7 +90,8 @@
         total = None
         for source in range(half):
             term = lax.dot_general(
-                held[far, head, source], feat[source], (((1,), (1,)), ((), ())), preferred_element_type=jnp.float32
+                held[far, head, source], columns_of(base + source), (((1,), (1,)), ((), ())),
+                preferred_element_type=jnp.float32,
             )
             total = term if total is None else total + term
         return total
@@ -255,9 +261,9 @@
         out[...] = value
 
 
-def params(collective_id):
+def params(collective_id, grant=32):
     return pltpu.CompilerParams(
-        collective_id=collective_id, has_side_effects=True, vmem_limit_bytes=32 * 2**20
+        collective_id=collective_id, has_side_effects=True, vmem_limit_bytes=grant * 2**20
     )
 
 
@@ -286,8 +292,7 @@
     draws = own * n
     mean_rows, scale_rows = mean_head.T, scale_head.T
     half = n // 2
-    my_half = lax.dynamic_slice_in_dim(features, lax.div(me, half) * (half * rows), half * rows, 1)
-    feat = my_half.reshape(batch, half, rows).transpose(1, 0, 2)
+    feat = features.reshape(batch, n, rows).transpose(1, 0, 2) if rows % 128 else features
 
     heads, noise_t = pl.pallas_call(
         functools.partial(exchange_kernel, n, units),
@@ -310,7 +315,7 @@
             pltpu.SemaphoreType.DMA((2, 2)),
             pltpu.SemaphoreType.DMA,
         ],
-        compiler_params=params(0),
+        compiler_params=params(0, 60),
     )(feat, mean_rows, scale_rows, noise.transpose(0, 2, 1))
 
     first = start_of(me, n, units) * UNIT
@@ -335,10 +340,11 @@
     lse = reduce_over(jnp.stack((local_top, local_total)), (ncls, n), True, 1)
     log_prob = logits - lse[:, None]
     best = jnp.max(log_prob, axis=0)
-    mix = best + jnp.log(jnp.sum(jnp.exp(log_prob - best[None]), axis=0))
-    ratio = jnp.exp(log_prob - mix[None])
-    label_dot = reduce_over(jnp.sum(my_labels[None] * ratio, axis=1), (ncls, n), False, 2)
-    logit_cot = (jnp.exp(log_prob) * label_dot[:, None] - my_labels[None] * ratio) / batch
+    risen = jnp.exp(log_prob - best[None])
+    inverse = 1.0 / jnp.sum(risen, axis=0)
+    weight = my_labels * inverse
+    label_dot = reduce_over(jnp.sum(weight[None] * risen, axis=1), (ncls, n), False, 2)
+    logit_cot = risen * ((jnp.exp(best) / batch)[None] * label_dot[:, None] - (weight / batch)[None])
     dmean = jnp.sum(logit_cot, axis=0)
     dspread = jnp.sum(logit_cot * lowrank, axis=0)
     cots = jnp.stack((dmean, dspread * jax.nn.sigmoid(scale_pre))).astype(jnp.bfloat16)

time: 149 us -> 149 us (level)
  local copies, waits for them, and re-layouts: 4.7 us -> 1.44 us
  Pallas kernels: 118 us -> 120 us
    unnamed x12 -> x9, local copies, waits for them, and re-layouts: 3.59 us -> 1.44 us
    pallas_call x1, Pallas kernels: 52.9 us -> 55 us  [on_device(): pl.pallas_call(functools.partial(exchange_kernel, n, units), out_shape=(j...]
where the time goes in v4:
time: 149 us
  Pallas kernels  120 us (81%)
  other arithmetic  14.6 us (10%)
  matrix products  9.22 us (6%)
  starting transfers between devices  3.09 us (2%)
    pallas_call x1, Pallas kernels, on_device(): pl.pallas_call(functools.partial(exchange_kernel, n, units), out_shape=(j...  55 us
    pallas_call x1, Pallas kernels, on_device(): pl.pallas_call(functools.partial(gather_kernel, n, units), out_shape=jax....  43.8 us
    pallas_call x2, Pallas kernels, reduce_over(): pl.pallas_call(functools.partial(reduce_kernel, counts, softmax), out_sha...  21 us
    reduce_sum x1, other arithmetic, on_device(): dmean = jnp.sum(logit_cot, axis=0)  3.31 us
    ppermute x2, starting transfers between devices, on_device(): lax.ppermute(feature_grad, 'cls', [(i, i ^ step) for i in range(ncls)])  3.09 us
  transfers between devices with their start and end apart: 2, of which 0 were waited for; matrix products, arithmetic and copies ran while one was open for 4% of the time, Pallas kernels for 0%

profile of v4, /device:TPU:9, one launch (start us, length us, event | category | flops | bytes accessed | tf_op | source)
XLA Modules:
  0.0 149.0 jit_solution(9801960465419455974)
XLA Ops:
  0.6 0.0 copy-start
  0.7 1.4 copy.11
  2.1 55.0 %shard_map.85 = (f32[2,688,128]{2,1,0:T(8,128)}, bf16[8,2,50,128]{3,2,1,0:T(8,128)(2,1)}) custom-call(bf16[128,1024]{1,0:T(8,128)(2,1)} %feat.1, bf16[5472,128]{1,0:T(8,128)(2,1)} %bitcast.68, bf16[5472,128]{1,0:T(8,128)(2,1)} %bitcast.67, bf16[2,50,128]{2,1,0:T(8,128)(2,1)} %bitcast.70), custom_call_target="tpu_custom_call" | custom-call | tf_op jit(solution)/shard_map/pallas_call | solution.py:297
  57.1 1.4 slice_bitcast_fusion
  58.5 2.5 %fusion.32 = (f32[16,128]{1,0:T(8,128)S(1)}, f32[16,128,688]{1,2,0:T(8,128)S(1)}) fusion(f32[688]{0:T(1024)S(1)} %fusion.28, f32[688,128]{1,0:T(8,128)S(1)} %get-tuple-element.12, f32[688,128]{1,0:T(8,128)S(1)} %get-tuple-element.11, pred[688]{0:T(1024)(128)(4,1)S(1)} %iota_compare_fusion, bf16[16,50,128]{2,1,0:T(8,128)(2,1)} %bitcast.73, ...), kind=kOutput, calls=%fused_computation.50 | convolution fusion | flops 147945472 | bytes 6644740 | tf_op jit(solution)/shard_map/rc,srb->scb/dot_general | solution.py:333
  60.9 1.8 %exponential_reduce_fusion = f32[16,128]{1,0:T(8,128)S(1)} fusion(f32[16,128]{1,0:T(8,128)S(1)} %get-tuple-element.13, f32[688]{0:T(1024)S(1)} %fusion.28, f32[16,128,688]{1,2,0:T(8,128)S(1)} %get-tuple-element.14, f32[688,128]{1,0:T(8,128)S(1)} %get-tuple-element.12, f32[688,128]{1,0:T(8,128)S(1)} %get-tuple-element.11, pred[688]{0:T(1024)(128)(4,1)S(1)} %iota_compare_fusion), kind=kLoop, calls=%fused_computation.9 | loop fusion | flops 8452096 | bytes 6360432 | tf_op jit(solution)/shard_map/reduce_sum | solution.py:339
  62.8 11.5 %shard_map.86 = f32[16,128]{1,0:T(8,128)S(1)} custom-call(f32[2,16,128]{2,1,0:T(8,128)S(1)} %pad_maximum_fusion.1.x), custom_call_target="tpu_custom_call" | custom-call | tf_op jit(solution)/shard_map/pallas_call | solution.py:272
  74.3 1.6 %subtract_reduce_fusion = f32[688,128]{1,0:T(8,128)S(1)} fusion(f32[16,128]{1,0:T(8,128)S(1)} %shard_map.86, f32[688]{0:T(1024)S(1)} %fusion.28, f32[16,128,688]{1,2,0:T(8,128)S(1)} %get-tuple-element.14, f32[688,128]{1,0:T(8,128)S(1)} %get-tuple-element.12, f32[688,128]{1,0:T(8,128)S(1)} %get-tuple-element.11, pred[688]{0:T(1024)(128)(4,1)S(1)} %iota_compare_fusion), kind=kLoop, calls=%fused_computation.10 | loop fusion | flops 8366080 | bytes 6704496 | tf_op jit(solution)/shard_map/reduce_max | solution.py:342
  75.9 2.2 %fusion.5 = f32[688,128]{1,0:T(8,128)S(1)} fusion(f32[688,128]{1,0:T(8,128)S(1)} %subtract_reduce_fusion, f32[16,128]{1,0:T(8,128)S(1)} %shard_map.86, f32[688]{0:T(1024)S(1)} %fusion.28, f32[16,128,688]{1,2,0:T(8,128)S(1)} %get-tuple-element.14, f32[688,128]{1,0:T(8,128)S(1)} %get-tuple-element.12, f32[688,128]{1,0:T(8,128)S(1)} %get-tuple-element.11, ...), kind=kLoop, calls=%fused_computation.12 | loop fusion | flops 9775104 | bytes 7056752 | tf_op jit(solution)/shard_map/reduce_sum | solution.py:344
  78.1 1.2 broadcast_multiply_fusion
  79.3 2.2 %multiply_reduce_fusion.x = f32[16,128]{1,0:T(8,128)S(1)} fusion(f32[688,128]{1,0:T(8,128)S(1)} %get-tuple-element.10, f32[688,128]{1,0:T(8,128)S(1)} %subtract_reduce_fusion, f32[16,128]{1,0:T(8,128)S(1)} %shard_map.86, f32[688]{0:T(1024)S(1)} %fusion.28, f32[16,128,688]{1,2,0:T(8,128)S(1)} %get-tuple-element.14, f32[688,128]{1,0:T(8,128)S(1)} %get-tuple-element.12, ...), kind=kLoop, calls=%fused_computation.7 | loop fusion | flops 11270144 | bytes 7064944 | tf_op jit(solution)/shard_map/reduce_sum | solution.py:346
  81.5 9.6 %shard_map.87 = f32[16,128]{1,0:T(8,128)S(1)} custom-call(f32[16,128]{1,0:T(8,128)S(1)} %multiply_reduce_fusion.x), custom_call_target="tpu_custom_call" | custom-call | tf_op jit(solution)/shard_map/pallas_call | solution.py:272
  91.1 0.0 copy-start.2
  91.1 3.3 %fusion.4 = (bf16[688,128]{1,0:T(8,128)(2,1)S(1)}, f32[688,128]{1,0:T(8,128)S(1)}) fusion(f32[688,128]{1,0:T(8,128)S(1)} %get-tuple-element.9, f32[16,128]{1,0:T(8,128)S(1)} %shard_map.87, f32[688,128]{1,0:T(8,128)S(1)} %get-tuple-element.15, f32[688,128]{1,0:T(8,128)S(1)} %subtract_reduce_fusion, f32[16,128]{1,0:T(8,128)S(1)} %shard_map.86, ...), kind=kLoop, calls=%fused_computation.11 | loop fusion | flops 16732160 | bytes 7945584 | tf_op jit(solution)/shard_map/reduce_sum | solution.py:348
  94.4 0.0 copy-start.3
  94.4 0.2 fusion.22
  94.6 43.8 %shard_map.88 = bf16[2,5472,128]{2,1,0:T(8,128)(2,1)S(1)} custom-call(bf16[2,688,128]{2,1,0:T(8,128)(2,1)S(1)} %pad_maximum_fusion.cot), custom_call_target="tpu_custom_call" | custom-call | tf_op jit(solution)/shard_map/pallas_call | solution.py:352
  138.5 0.6 fusion.6
  139.0 0.6 fusion.18
  139.6 1.8 %collective-permute-start = (f32[128,128]{1,0:T(8,128)S(1)}, f32[128,128]{1,0:T(8,128)S(1)}, u32[]{:S(2)}, u32[]{:S(2)}) collective-permute-start(f32[128,128]{1,0:T(8,128)S(1)} %fusion.18), channel_id=1, source_target_pairs={{0,8},{8,0},{16,24},{24,16},{1,9},{9,1},{17,25},{25,17},{2,10},{10... | collective-permute-start | bytes 196616 | tf_op jit(solution)/shard_map/ppermute | solution.py:374
  141.4 2.8 %fusion.8 = f32[128,5472]{0,1:T(8,128)} fusion(bf16[2,5472,128]{2,1,0:T(8,128)(2,1)S(1)} %shard_map.88, bf16[128,1024]{1,0:T(8,128)(2,1)} %feat.1, s32[]{:T(128)S(6)} %select_n.38), kind=kOutput, calls=%fused_computation.15 | convolution fusion | flops 179306496 | bytes 4235268 | tf_op jit(solution)/shard_map/dot_general | solution.py:371
  144.3 1.3 collective-permute-start.1
  145.5 2.8 %fusion.12 = f32[128,5472]{0,1:T(8,128)} fusion(bf16[2,5472,128]{2,1,0:T(8,128)(2,1)S(1)} %shard_map.88, bf16[128,1024]{1,0:T(8,128)(2,1)} %feat.1, s32[]{:T(128)S(6)} %select_n.38), kind=kOutput, calls=%fused_computation.19 | convolution fusion | flops 179306496 | bytes 4235268 | tf_op jit(solution)/shard_map/dot_general | solution.py:370
  148.4 0.6 add.66
  (12 shorter events, 0.1 us)
Async XLA Ops:
  0.6 57.8 %copy-start = (bf16[5472,50]{0,1:T(8,128)(2,1)S(1)}, bf16[5472,50]{0,1:T(8,128)(2,1)}, u32[]{:S(2)}) copy-start(bf16[5472,50]{0,1:T(8,128)(2,1)} %param.9) | copy-start | bytes 1641604
  81.5 12.9 %copy-start.1 = (f32[2,688,128]{2,1,0:T(8,128)S(1)}, f32[2,688,128]{2,1,0:T(8,128)}, u32[]{:S(2)}) copy-start(f32[2,688,128]{2,1,0:T(8,128)} %get-tuple-element.5) | copy-start | bytes 2113540
  91.1 47.4 %copy-start.2 = (bf16[128,5472]{0,1:T(8,128)(2,1)S(1)}, bf16[128,5472]{0,1:T(8,128)(2,1)}, u32[]{:S(2)}) copy-start(bf16[128,5472]{0,1:T(8,128)(2,1)} %param.8) | copy-start | bytes 4202500
  94.4 44.6 %copy-start.3 = (bf16[128,5472]{0,1:T(8,128)(2,1)S(1)}, bf16[128,5472]{0,1:T(8,128)(2,1)}, u32[]{:S(2)}) copy-start(bf16[128,5472]{0,1:T(8,128)(2,1)} %param.7) | copy-start | bytes 4202500
  139.6 4.6 %collective-permute-start = (f32[128,128]{1,0:T(8,128)S(1)}, f32[128,128]{1,0:T(8,128)S(1)}, u32[]{:S(2)}, u32[]{:S(2)}) collective-permute-start(f32[128,128]{1,0:T(8,128)S(1)} %fusion.18), channel_id=1, source_target_pairs={{0,8},{8,0},{16,24},{24,16},{1,9},{9,1},{17,25},{25,17},{2,10},{10... | collective-permute-start | bytes 196616 | tf_op jit(solution)/shard_map/ppermute | solution.py:374
  144.3 4.1 %collective-permute-start.1 = (f32[128,128]{1,0:T(8,128)S(1)}, f32[128,128]{1,0:T(8,128)S(1)}, u32[]{:S(2)}, u32[]{:S(2)}) collective-permute-start(f32[128,128]{1,0:T(8,128)S(1)} %add.65), channel_id=1, source_target_pairs={{0,16},{8,24},{16,0},{24,8},{1,17},{9,25},{17,1},{25,9},{2,18},{10... | collective-permute-start | bytes 196616 | tf_op jit(solution)/shard_map/ppermute | solution.py:374

commit v5 on v4

--- a/solution.py
+++ b/solution.py
@@ -315,7 +315,7 @@
             pltpu.SemaphoreType.DMA((2, 2)),
             pltpu.SemaphoreType.DMA,
         ],
-        compiler_params=params(0, 60),
+        compiler_params=params(0),
     )(feat, mean_rows, scale_rows, noise.transpose(0, 2, 1))
 
     first = start_of(me, n, units) * UNIT

time: 149 us -> 148 us (level)
  local copies, waits for them, and re-layouts: 1.44 us -> 4.46 us
  Pallas kernels: 120 us -> 118 us
    unnamed x9 -> x11, local copies, waits for them, and re-layouts: 1.44 us -> 4.46 us
    pallas_call x1, Pallas kernels: 55 us -> 52.9 us  [on_device(): pl.pallas_call(functools.partial(exchange_kernel, n, units), out_shape=(j...]
where the time goes in v5:
time: 148 us
  Pallas kernels  118 us (80%)
  other arithmetic  13.5 us (9%)
  matrix products  8.32 us (6%)
  local copies, waits for them, and re-layouts  4.46 us (3%)
  starting transfers between devices  3.09 us (2%)
    pallas_call x1, Pallas kernels, on_device(): pl.pallas_call(functools.partial(exchange_kernel, n, units), out_shape=(j...  52.9 us
    pallas_call x1, Pallas kernels, on_device(): pl.pallas_call(functools.partial(gather_kernel, n, units), out_shape=jax....  43.8 us
    pallas_call x2, Pallas kernels, reduce_over(): pl.pallas_call(functools.partial(reduce_kernel, counts, softmax), out_sha...  21 us
    unnamed x11, local copies, waits for them, and re-layouts  4.46 us
    reduce_sum x1, other arithmetic, on_device(): dmean = jnp.sum(logit_cot, axis=0)  3.3 us
    ppermute x2, starting transfers between devices, on_device(): lax.ppermute(feature_grad, 'cls', [(i, i ^ step) for i in range(ncls)])  3.09 us
  transfers between devices with their start and end apart: 2, of which 0 were waited for; matrix products, arithmetic and copies ran while one was open for 4% of the time, Pallas kernels for 0%

profile of v5, /device:TPU:9, one launch (start us, length us, event | category | flops | bytes accessed | tf_op | source)
XLA Modules:
  0.0 148.0 jit_solution(16841613516120629872)
XLA Ops:
  0.7 0.8 copy.11
  1.5 1.3 copy-done.1
  2.8 1.3 copy-done.2
  4.2 0.9 copy-done.4
  5.1 52.9 %shard_map.85 = (f32[2,688,128]{2,1,0:T(8,128)S(1)}, bf16[8,2,50,128]{3,2,1,0:T(8,128)(2,1)S(1)}) custom-call(bf16[128,1024]{1,0:T(8,128)(2,1)S(1)} %copy-done.4, bf16[5472,128]{1,0:T(8,128)(2,1)S(1)} %bitcast.68, bf16[5472,128]{1,0:T(8,128)(2,1)S(1)} %bitcast.67, bf16[2,50,128]{2,1,0:T(8,128)(2,1)S(1)} %bitcast.69), custom_call_target="tpu_custom_call" | custom-call | tf_op jit(solution)/shard_map/pallas_call | solution.py:297
  58.1 0.3 slice_bitcast_fusion
  58.4 1.5 %fusion.32 = (f32[16,128]{1,0:T(8,128)S(1)}, f32[16,128,688]{1,2,0:T(8,128)S(1)}) fusion(f32[688]{0:T(1024)S(1)} %fusion.28, f32[688,128]{1,0:T(8,128)S(1)} %get-tuple-element.12, f32[688,128]{1,0:T(8,128)S(1)} %get-tuple-element.11, pred[688]{0:T(1024)(128)(4,1)S(1)} %iota_compare_fusion, bf16[16,50,128]{2,1,0:T(8,128)(2,1)S(1)} %bitcast.70, ...), kind=kOutput, calls=%fused_computation.50 | convolution fusion | flops 147945472 | bytes 6669316 | tf_op jit(solution)/shard_map/rc,srb->scb/dot_general | solution.py:333
  59.9 1.8 %exponential_reduce_fusion = f32[16,128]{1,0:T(8,128)S(1)} fusion(f32[16,128]{1,0:T(8,128)S(1)} %get-tuple-element.13, f32[688]{0:T(1024)S(1)} %fusion.28, f32[16,128,688]{1,2,0:T(8,128)S(1)} %get-tuple-element.14, f32[688,128]{1,0:T(8,128)S(1)} %get-tuple-element.12, f32[688,128]{1,0:T(8,128)S(1)} %get-tuple-element.11, pred[688]{0:T(1024)(128)(4,1)S(1)} %iota_compare_fusion), kind=kLoop, calls=%fused_computation.9 | loop fusion | flops 8452096 | bytes 6360432 | tf_op jit(solution)/shard_map/reduce_sum | solution.py:339
  61.8 11.5 %shard_map.86 = f32[16,128]{1,0:T(8,128)S(1)} custom-call(f32[2,16,128]{2,1,0:T(8,128)S(1)} %pad_maximum_fusion.1.x), custom_call_target="tpu_custom_call" | custom-call | tf_op jit(solution)/shard_map/pallas_call | solution.py:272
  73.3 1.6 %subtract_reduce_fusion = f32[688,128]{1,0:T(8,128)S(1)} fusion(f32[16,128]{1,0:T(8,128)S(1)} %shard_map.86, f32[688]{0:T(1024)S(1)} %fusion.28, f32[16,128,688]{1,2,0:T(8,128)S(1)} %get-tuple-element.14, f32[688,128]{1,0:T(8,128)S(1)} %get-tuple-element.12, f32[688,128]{1,0:T(8,128)S(1)} %get-tuple-element.11, pred[688]{0:T(1024)(128)(4,1)S(1)} %iota_compare_fusion), kind=kLoop, calls=%fused_computation.10 | loop fusion | flops 8366080 | bytes 6704496 | tf_op jit(solution)/shard_map/reduce_max | solution.py:342
  74.9 2.2 %fusion.5 = f32[688,128]{1,0:T(8,128)S(1)} fusion(f32[688,128]{1,0:T(8,128)S(1)} %subtract_reduce_fusion, f32[16,128]{1,0:T(8,128)S(1)} %shard_map.86, f32[688]{0:T(1024)S(1)} %fusion.28, f32[16,128,688]{1,2,0:T(8,128)S(1)} %get-tuple-element.14, f32[688,128]{1,0:T(8,128)S(1)} %get-tuple-element.12, f32[688,128]{1,0:T(8,128)S(1)} %get-tuple-element.11, ...), kind=kLoop, calls=%fused_computation.12 | loop fusion | flops 9775104 | bytes 7056752 | tf_op jit(solution)/shard_map/reduce_sum | solution.py:344
  77.1 1.2 broadcast_multiply_fusion
  78.3 2.2 %multiply_reduce_fusion.x = f32[16,128]{1,0:T(8,128)S(1)} fusion(f32[688,128]{1,0:T(8,128)S(1)} %get-tuple-element.10, f32[688,128]{1,0:T(8,128)S(1)} %subtract_reduce_fusion, f32[16,128]{1,0:T(8,128)S(1)} %shard_map.86, f32[688]{0:T(1024)S(1)} %fusion.28, f32[16,128,688]{1,2,0:T(8,128)S(1)} %get-tuple-element.14, f32[688,128]{1,0:T(8,128)S(1)} %get-tuple-element.12, ...), kind=kLoop, calls=%fused_computation.7 | loop fusion | flops 11270144 | bytes 7064944 | tf_op jit(solution)/shard_map/reduce_sum | solution.py:346
  80.5 9.6 %shard_map.87 = f32[16,128]{1,0:T(8,128)S(1)} custom-call(f32[16,128]{1,0:T(8,128)S(1)} %multiply_reduce_fusion.x), custom_call_target="tpu_custom_call" | custom-call | tf_op jit(solution)/shard_map/pallas_call | solution.py:272
  90.1 3.3 %fusion.4 = (bf16[688,128]{1,0:T(8,128)(2,1)S(1)}, f32[688,128]{1,0:T(8,128)S(1)}) fusion(f32[688,128]{1,0:T(8,128)S(1)} %get-tuple-element.9, f32[16,128]{1,0:T(8,128)S(1)} %shard_map.87, f32[688,128]{1,0:T(8,128)S(1)} %get-tuple-element.15, f32[688,128]{1,0:T(8,128)S(1)} %subtract_reduce_fusion, f32[16,128]{1,0:T(8,128)S(1)} %shard_map.86, ...), kind=kLoop, calls=%fused_computation.11 | loop fusion | flops 16732160 | bytes 7945584 | tf_op jit(solution)/shard_map/reduce_sum | solution.py:348
  93.4 0.2 fusion.22
  93.6 43.8 %shard_map.88 = bf16[2,5472,128]{2,1,0:T(8,128)(2,1)S(1)} custom-call(bf16[2,688,128]{2,1,0:T(8,128)(2,1)S(1)} %pad_maximum_fusion.cot), custom_call_target="tpu_custom_call" | custom-call | tf_op jit(solution)/shard_map/pallas_call | solution.py:352
  137.4 0.6 fusion.6
  138.0 0.6 fusion.18
  138.6 1.8 %collective-permute-start = (f32[128,128]{1,0:T(8,128)S(1)}, f32[128,128]{1,0:T(8,128)S(1)}, u32[]{:S(2)}, u32[]{:S(2)}) collective-permute-start(f32[128,128]{1,0:T(8,128)S(1)} %fusion.18), channel_id=1, source_target_pairs={{0,8},{8,0},{16,24},{24,16},{1,9},{9,1},{17,25},{25,17},{2,10},{10... | collective-permute-start | bytes 196616 | tf_op jit(solution)/shard_map/ppermute | solution.py:374
  140.4 2.8 %fusion.8 = f32[128,5472]{0,1:T(8,128)} fusion(bf16[2,5472,128]{2,1,0:T(8,128)(2,1)S(1)} %shard_map.88, bf16[128,1024]{1,0:T(8,128)(2,1)} %feat.1, s32[]{:T(128)S(6)} %select_n.38), kind=kOutput, calls=%fused_computation.15 | convolution fusion | flops 179306496 | bytes 4235268 | tf_op jit(solution)/shard_map/dot_general | solution.py:371
  143.2 1.3 collective-permute-start.1
  144.5 2.8 %fusion.12 = f32[128,5472]{0,1:T(8,128)} fusion(bf16[2,5472,128]{2,1,0:T(8,128)(2,1)S(1)} %shard_map.88, bf16[128,1024]{1,0:T(8,128)(2,1)} %feat.1, s32[]{:T(128)S(6)} %select_n.38), kind=kOutput, calls=%fused_computation.19 | convolution fusion | flops 179306496 | bytes 4235268 | tf_op jit(solution)/shard_map/dot_general | solution.py:370
  147.3 0.6 add.66
  (14 shorter events, 0.1 us)
Async XLA Ops:
  0.6 57.8 %copy-start = (bf16[5472,50]{0,1:T(8,128)(2,1)S(1)}, bf16[5472,50]{0,1:T(8,128)(2,1)}, u32[]{:S(2)}) copy-start(bf16[5472,50]{0,1:T(8,128)(2,1)} %param.9) | copy-start | bytes 1641604
  1.5 1.3 copy-start.1
  2.8 1.3 copy-start.2
  4.2 0.9 copy-start.4
  93.4 44.6 %copy-start.3 = (bf16[128,5472]{0,1:T(8,128)(2,1)S(1)}, bf16[128,5472]{0,1:T(8,128)(2,1)}, u32[]{:S(2)}) copy-start(bf16[128,5472]{0,1:T(8,128)(2,1)} %param.7) | copy-start | bytes 4202500
  138.6 4.6 %collective-permute-start = (f32[128,128]{1,0:T(8,128)S(1)}, f32[128,128]{1,0:T(8,128)S(1)}, u32[]{:S(2)}, u32[]{:S(2)}) collective-permute-start(f32[128,128]{1,0:T(8,128)S(1)} %fusion.18), channel_id=1, source_target_pairs={{0,8},{8,0},{16,24},{24,16},{1,9},{9,1},{17,25},{25,17},{2,10},{10... | collective-permute-start | bytes 196616 | tf_op jit(solution)/shard_map/ppermute | solution.py:374
  143.2 4.1 %collective-permute-start.1 = (f32[128,128]{1,0:T(8,128)S(1)}, f32[128,128]{1,0:T(8,128)S(1)}, u32[]{:S(2)}, u32[]{:S(2)}) collective-permute-start(f32[128,128]{1,0:T(8,128)S(1)} %add.65), channel_id=1, source_target_pairs={{0,16},{8,24},{16,0},{24,8},{1,17},{9,25},{17,1},{25,9},{2,18},{10... | collective-permute-start | bytes 196616 | tf_op jit(solution)/shard_map/ppermute | solution.py:374
